TPU v7x, 32 devices: a whole 2x2x4 slice. The times are simulated.
32 devices in a mesh: grp: 4 (over y, x), blk: 8 (over z, core).
Axes of the slice: x: 2, y: 2, z: 4, core: 2. Of those that a mesh axis runs over, the one named last changes fastest.
Arguments:
- estimate: float32 [32, 256, 256], P('blk'), may hold values from 0.25 to 4
- measured: bfloat16 [6, 256, 32, 256], P(None, 'blk'), may hold values from 0.25 to 4
- tile_plane: int32 [6, 256], P(None, 'blk'), may hold values from 0 to 31, as said below
- tile_strip: int32 [6, 256], P(None, 'blk'), may hold values from 0 to 7, as said below
- view_group: int32 [6], replicated, may hold values from 0 to 3, as said below
- kernel_cols: float32 [6, 3, 31], replicated, may hold values from 0.002 to 0.1
- kernel_rows: float32 [6, 3, 31], replicated, may hold values from 0.002 to 0.1
- kernel_planes: float32 [6, 3, 31], replicated, may hold values from 0.002 to 0.1
Outputs:
- updated: float32 [32, 256, 256], P('blk')
Inputs may be any that keep to these rules, and one draw needn't show every extreme that they name: For each view the pairs (tile_plane, tile_strip) name every plane and strip exactly once; the 32 tiles of one view on one device of blk hold exactly 4 tiles of every block of 4 consecutive planes and exactly 4 tiles of every strip. `tile_strip`: see tile_plane. `view_group`: every group has at least one view and at most 2; some group has exactly 2.
All inputs are finite; a program needn't handle non-finite values.
Results may differ from a plain program's by a relative error of at most 0.0003.
Values may be sent and summed in bfloat16 or wider, within the bound.
A program may use at most 128 MiB of HBM per device.

v0:
```python
import jax
import jax.numpy as jnp
from jax import lax
from jax.sharding import PartitionSpec as P

VSLOT = 2


def banded(taps, length):
    width = taps.shape[-1]
    half = width // 2
    position = jnp.arange(length, dtype=jnp.int32)
    offsets = position[None, :] - position[:, None] + half
    onehot = (offsets[:, :, None] == jnp.arange(width, dtype=jnp.int32)[None, None, :]).astype(
        jnp.float32
    )
    return jnp.einsum("imt,rt->rim", onehot, taps, precision=lax.Precision.HIGHEST)


def send_order(owner, per_owner, owners):
    hits = (owner[:, None] == jnp.arange(owners, dtype=jnp.int32)[None, :]).astype(jnp.int32)
    before = jnp.cumsum(hits, axis=0) - hits
    return owner * per_owner + jnp.sum(before * hits, axis=1)


def shards(
    estimate, measured, tile_plane, tile_strip, view_group, kernel_cols, kernel_rows, kernel_planes
):
    highest = lax.Precision.HIGHEST
    plane_count, row_count, col_count = estimate.shape
    blocks = lax.axis_size("blk")
    planes_all = plane_count * blocks
    strip_rows = row_count // blocks
    group_index = lax.axis_index("grp")
    view_count = view_group.shape[0]
    matches = (view_group == group_index).astype(jnp.int32)
    ranking = jnp.cumsum(matches) - matches
    members = jnp.sum(matches).astype(jnp.float32)
    view_ids = jnp.arange(view_count, dtype=jnp.int32)
    summed_factor = None
    for slot_index in range(VSLOT):
        picked = matches * (ranking == slot_index).astype(jnp.int32)
        is_live = jnp.sum(picked).astype(jnp.float32)
        chosen = jnp.sum(picked * view_ids)
        pieces = measured[chosen]
        planes = tile_plane[chosen]
        strips = tile_strip[chosen]
        band_cols = banded(kernel_cols[chosen], col_count)
        band_rows = banded(kernel_rows[chosen], row_count)
        band_planes = banded(kernel_planes[chosen], planes_all)
        rank_terms = jnp.einsum("zym,rim->rzyi", estimate, band_cols, precision=highest)
        rank_terms = jnp.einsum("rzmx,rim->rzix", rank_terms, band_rows, precision=highest)
        pencil_terms = lax.all_to_all(rank_terms, "blk", split_axis=2, concat_axis=1, tiled=True)
        blurred = jnp.einsum("rmyx,rim->iyx", pencil_terms, band_planes, precision=highest)
        positions = send_order(strips, plane_count, blocks)
        outgoing = (
            jnp.zeros_like(pieces).at[positions].set(pieces),
            jnp.zeros_like(planes).at[positions].set(planes),
            jnp.zeros_like(strips).at[positions].set(strips),
        )
        got_pieces, got_planes, got_strips = (
            lax.all_to_all(outgoing[0], "blk", split_axis=0, concat_axis=0, tiled=True),
            lax.all_to_all(outgoing[1], "blk", split_axis=0, concat_axis=0, tiled=True),
            lax.all_to_all(outgoing[2], "blk", split_axis=0, concat_axis=0, tiled=True),
        )
        observed = (
            jnp.zeros((planes_all, strip_rows, col_count), jnp.bfloat16)
            .at[got_planes]
            .set(got_pieces)
        )
        ratios = observed.astype(jnp.float32) / blurred
        adjoint = jnp.einsum("iyx,rim->rmyx", ratios, band_planes, precision=highest)
        adjoint = lax.all_to_all(adjoint, "blk", split_axis=1, concat_axis=2, tiled=True)
        adjoint = jnp.einsum("rzix,rim->rzmx", adjoint, band_rows, precision=highest)
        factor = jnp.einsum("rzyi,rim->zym", adjoint, band_cols, precision=highest)
        weighted = is_live * factor
        summed_factor = weighted if summed_factor is None else summed_factor + weighted
    average = summed_factor / members
    log_mean = jnp.log(average)
    summed_logs = lax.psum(log_mean, "grp")
    return estimate * jnp.exp(summed_logs / lax.axis_size("grp"))


def solution(mesh):
    in_specs = (
        P("blk", None, None),
        P(None, "blk", None, None),
        P(None, "blk"),
        P(None, "blk"),
        P(),
        P(),
        P(),
        P(),
    )
    out_specs = P("blk", None, None)
    return jax.shard_map(shards, mesh=mesh, in_specs=in_specs, out_specs=out_specs, check_vma=False)
```

profile of v0, /device:TPU:0, one launch (start us, length us, event | category | flops | bytes accessed | tf_op | source)
XLA Modules:
  0.0 457.7 jit_solution(15087829654246292614)
XLA Ops:
  7.4 1.4 fusion.117
  16.4 6.4 %all-to-all-start.4 = ((s32[8,4,1]{1,2,0:T(1,128)}), s32[8,4,1]{1,2,0:T(1,128)S(1)}, u32[]{:S(2)}, u32[]{:S(2)}) async-start(s32[8,4,1]{1,2,0:T(1,128)} %bitcast.49), calls=%async_computation.4 | async-start | bytes 8192 | tf_op jit(solution)/shard_map/all_to_all | solution.py:63
  25.4 2.9 all-to-all-done.4
  28.2 3.3 all-to-all-start
  32.4 4.4 scatter_fusion.2
  37.1 4.7 %all-to-all-start.5 = ((bf16[32,32,256]{2,1,0:T(8,128)(2,1)}), bf16[32,32,256]{2,1,0:T(8,128)(2,1)S(1)}, u32[]{:S(2)}, u32[]{:S(2)}) async-start(bf16[32,32,256]{2,1,0:T(8,128)(2,1)} %scatter_fusion.2), calls=%async_computation.5 | async-start | bytes 1048576 | tf_op jit(solution)/shard_map/all_to_all | solution.py:62
  42.7 4.3 scatter_fusion
  47.1 2.7 fusion
  49.8 7.4 %all-to-all-done.5 = bf16[32,32,256]{2,1,0:T(8,128)(2,1)S(1)} async-done(((bf16[32,32,256]{2,1,0:T(8,128)(2,1)}), bf16[32,32,256]{2,1,0:T(8,128)(2,1)S(1)}, u32[]{:S(2)}, u32[]{:S(2)}) %all-to-all-start.5) | async-done | bytes 524320 | tf_op jit(solution)/shard_map/all_to_all | solution.py:62
  58.0 3.7 all-to-all-start.1
  61.7 3.4 fusion.1
  65.1 2.8 fusion.61
  67.9 3.0 fusion.27
  70.9 3.7 copy.75
  74.6 2.3 all-to-all-done.1
  77.7 4.1 all-to-all-start.6
  81.8 2.7 fusion.2
  84.5 3.4 fusion.3
  87.9 2.8 fusion.63
  90.8 3.0 fusion.24
  93.8 3.9 copy.58
  97.6 55.2 %all-to-all-done.6 = f32[3,4,256,256]{3,1,0,2:T(4,128)S(1)} async-done(((f32[3,4,256,256]{3,1,0,2:T(4,128)}), f32[3,4,256,256]{3,1,0,2:T(4,128)S(1)}, u32[]{:S(2)}, u32[]{:S(2)}) %all-to-all-start.6) | async-done | bytes 3145760 | tf_op jit(solution)/shard_map/all_to_all | solution.py:53
  152.8 1.7 copy-done.2
  154.5 3.6 all-to-all-start.2
  158.2 1.9 fusion.81
  162.2 4.8 %scatter_fusion.3 = bf16[32,32,256]{2,1,0:T(8,128)(2,1)} fusion(bf16[32,32,256]{2,1,0:T(8,128)(2,1)} %broadcast.127.clone, s32[32]{0:T(128)S(1)} %fusion.108, bf16[32,32,256]{2,1,0:T(8,128)(2,1)} %copy-done.19), kind=kCustom, calls=%fused_computation.5 | custom fusion | bytes 1572992 | tf_op jit(solution)/shard_map/scatter | solution.py:69
  167.0 2.4 copy.76
  169.9 3.9 fusion.33
  173.9 2.8 fusion.57
  176.6 3.5 copy.81
  180.2 49.5 %all-to-all-done.2 = f32[3,4,256,256]{3,1,0,2:T(4,128)S(1)} async-done(((f32[3,4,256,256]{3,1,0,2:T(4,128)}), f32[3,4,256,256]{3,1,0,2:T(4,128)S(1)}, u32[]{:S(2)}, u32[]{:S(2)}) %all-to-all-start.2) | async-done | bytes 3145760 | tf_op jit(solution)/shard_map/all_to_all | solution.py:53
  229.6 4.6 %all-to-all-start.7 = ((f32[3,32,32,256]{3,2,0,1:T(8,128)}), f32[3,32,32,256]{3,2,0,1:T(8,128)}, u32[]{:S(2)}, u32[]{:S(2)}) async-start(f32[3,32,32,256]{3,2,0,1:T(8,128)} %copy.81), calls=%async_computation.7 | async-start | bytes 6291456 | tf_op jit(solution)/shard_map/all_to_all | solution.py:73
  234.3 1.9 fusion.82
  237.8 4.8 %scatter_fusion.1 = bf16[32,32,256]{2,1,0:T(8,128)(2,1)} fusion(bf16[32,32,256]{2,1,0:T(8,128)(2,1)} %broadcast.127.clone.2, s32[32]{0:T(128)S(1)} %fusion.106, bf16[32,32,256]{2,1,0:T(8,128)(2,1)} %copy-done.18), kind=kCustom, calls=%fused_computation.2 | custom fusion | bytes 1572992 | tf_op jit(solution)/shard_map/scatter | solution.py:69
  243.6 3.9 fusion.30
  247.5 2.8 fusion.59
  250.3 3.5 copy.64
  253.8 52.0 %all-to-all-done.7 = f32[3,32,32,256]{3,2,0,1:T(8,128)} async-done(((f32[3,32,32,256]{3,2,0,1:T(8,128)}), f32[3,32,32,256]{3,2,0,1:T(8,128)}, u32[]{:S(2)}, u32[]{:S(2)}) %all-to-all-start.7) | async-done | bytes 3145760 | tf_op jit(solution)/shard_map/all_to_all | solution.py:73
  305.8 4.4 all-to-all-start.3
  314.9 2.1 copy.83
  317.0 64.7 %all-to-all-done.3 = f32[3,32,32,256]{3,2,0,1:T(8,128)} async-done(((f32[3,32,32,256]{3,2,0,1:T(8,128)}), f32[3,32,32,256]{3,2,0,1:T(8,128)}, u32[]{:S(2)}, u32[]{:S(2)}) %all-to-all-start.3) | async-done | bytes 3145760 | tf_op jit(solution)/shard_map/all_to_all | solution.py:73
  381.7 2.3 copy.66
  384.1 3.0 fusion.16
  387.1 2.6 fusion.54
  389.8 3.0 fusion.20
  392.8 3.7 fusion.48
  396.5 51.5 %all-reduce.2.cloned.1.call-done = f32[4,256,256]{2,1,0:T(8,128)} async-done(((f32[4,256,256]{2,1,0:T(8,128)}), f32[4,256,256]{2,1,0:T(8,128)}) %all-reduce.2.cloned.1.call-update) | async-done | bytes 1048592 | tf_op jit(solution)/shard_map/psum | solution.py:80
  448.0 2.4 exponential_multiply_fusion
  (75 shorter events, 18.6 us)
Async XLA Ops:
  6.5 40.5 %copy-start = (f32[6,3,31]{2,1,0:T(4,128)S(1)}, f32[6,3,31]{2,1,0:T(4,128)}, u32[]{:S(2)}) copy-start(f32[6,3,31]{2,1,0:T(4,128)} %param.13) | copy-start | bytes 6700
  16.4 11.9 %all-to-all-start.4 = ((s32[8,4,1]{1,2,0:T(1,128)}), s32[8,4,1]{1,2,0:T(1,128)S(1)}, u32[]{:S(2)}, u32[]{:S(2)}) async-start(s32[8,4,1]{1,2,0:T(1,128)} %bitcast.49), calls=%async_computation.4 | async-start | bytes 8192 | tf_op jit(solution)/shard_map/all_to_all | solution.py:63
  28.2 8.9 %all-to-all-start = ((s32[8,4,1]{1,2,0:T(1,128)}), s32[8,4,1]{1,2,0:T(1,128)S(1)}, u32[]{:S(2)}, u32[]{:S(2)}) async-start(s32[8,4,1]{1,2,0:T(1,128)} %bitcast.13), calls=%async_computation | async-start | bytes 8192 | tf_op jit(solution)/shard_map/all_to_all | solution.py:63
  37.1 20.1 %all-to-all-start.5 = ((bf16[32,32,256]{2,1,0:T(8,128)(2,1)}), bf16[32,32,256]{2,1,0:T(8,128)(2,1)S(1)}, u32[]{:S(2)}, u32[]{:S(2)}) async-start(bf16[32,32,256]{2,1,0:T(8,128)(2,1)} %scatter_fusion.2), calls=%async_computation.5 | async-start | bytes 1048576 | tf_op jit(solution)/shard_map/all_to_all | solution.py:62
  42.7 22.4 %copy-start.3 = (f32[4,256,256]{2,1,0:T(8,128)S(1)}, f32[4,256,256]{2,1,0:T(8,128)}, u32[]{:S(2)}) copy-start(f32[4,256,256]{2,1,0:T(8,128)} %param.8) | copy-start | bytes 3145732
  49.7 18.2 %copy-start.12 = (f32[3,256,256]{2,0,1:T(4,128)}, f32[3,256,256]{2,0,1:T(4,128)S(1)}, u32[]{:S(2)}) copy-start(f32[3,256,256]{2,0,1:T(4,128)S(1)} %fusion) | copy-start | bytes 2359300
  57.2 0.8 copy-start.19
  58.0 19.0 %all-to-all-start.1 = ((bf16[32,32,256]{2,1,0:T(8,128)(2,1)}), bf16[32,32,256]{2,1,0:T(8,128)(2,1)S(1)}, u32[]{:S(2)}, u32[]{:S(2)}) async-start(bf16[32,32,256]{2,1,0:T(8,128)(2,1)} %scatter_fusion), calls=%async_computation.1 | async-start | bytes 1048576 | tf_op jit(solution)/shard_map/all_to_all | solution.py:62
  65.1 2.9 copy-start.8
  76.9 0.8 copy-start.18
  77.7 75.1 %all-to-all-start.6 = ((f32[3,4,256,256]{3,1,0,2:T(4,128)}), f32[3,4,256,256]{3,1,0,2:T(4,128)S(1)}, u32[]{:S(2)}, u32[]{:S(2)}) async-start(f32[3,4,256,256]{3,1,0,2:T(4,128)} %copy.75), calls=%async_computation.6 | async-start | bytes 6291456 | tf_op jit(solution)/shard_map/all_to_all | solution.py:53
  81.8 6.1 %copy-start.4 = (f32[4,256,256]{2,1,0:T(8,128)S(1)}, f32[4,256,256]{2,1,0:T(8,128)}, u32[]{:S(2)}) copy-start(f32[4,256,256]{2,1,0:T(8,128)} %param.8) | copy-start | bytes 3145732
  84.5 6.3 %copy-start.14 = (f32[3,256,256]{2,0,1:T(4,128)}, f32[3,256,256]{2,0,1:T(4,128)S(1)}, u32[]{:S(2)}) copy-start(f32[3,256,256]{2,0,1:T(4,128)S(1)} %fusion.2) | copy-start | bytes 2359300
  87.9 2.9 copy-start.10
  152.8 1.7 copy-start.2
  154.5 75.1 %all-to-all-start.2 = ((f32[3,4,256,256]{3,1,0,2:T(4,128)}), f32[3,4,256,256]{3,1,0,2:T(4,128)S(1)}, u32[]{:S(2)}, u32[]{:S(2)}) async-start(f32[3,4,256,256]{3,1,0,2:T(4,128)} %copy.58), calls=%async_computation.2 | async-start | bytes 6291456 | tf_op jit(solution)/shard_map/all_to_all | solution.py:53
  169.9 3.9 copy-start.7
  229.6 76.2 %all-to-all-start.7 = ((f32[3,32,32,256]{3,2,0,1:T(8,128)}), f32[3,32,32,256]{3,2,0,1:T(8,128)}, u32[]{:S(2)}, u32[]{:S(2)}) async-start(f32[3,32,32,256]{3,2,0,1:T(8,128)} %copy.81), calls=%async_computation.7 | async-start | bytes 6291456 | tf_op jit(solution)/shard_map/all_to_all | solution.py:73
  243.6 3.9 copy-start.6
  253.8 56.7 %copy-start.9 = (f32[3,256,256]{2,0,1:T(4,128)S(1)}, f32[3,256,256]{2,0,1:T(4,128)}, u32[]{:S(2)}) copy-start(f32[3,256,256]{2,0,1:T(4,128)} %copy-done.8) | copy-start | bytes 2359300
  253.8 57.9 %copy-start.11 = (f32[3,256,256]{2,0,1:T(4,128)S(1)}, f32[3,256,256]{2,0,1:T(4,128)}, u32[]{:S(2)}) copy-start(f32[3,256,256]{2,0,1:T(4,128)} %copy-done.10) | copy-start | bytes 2359300
  305.8 76.0 %all-to-all-start.3 = ((f32[3,32,32,256]{3,2,0,1:T(8,128)}), f32[3,32,32,256]{3,2,0,1:T(8,128)}, u32[]{:S(2)}, u32[]{:S(2)}) async-start(f32[3,32,32,256]{3,2,0,1:T(8,128)} %copy.64), calls=%async_computation.3 | async-start | bytes 6291456 | tf_op jit(solution)/shard_map/all_to_all | solution.py:73
  310.2 137.8 %all-reduce.2.cloned.1.call-start = ((), (), s32[]{:S(2)}) async-start(), calls=%async_computation.8 | async-start | bytes 2097152 | tf_op jit(solution)/shard_map/psum | solution.py:80
  381.7 2.3 copy-start.17
  384.1 3.0 copy-start.13
  387.1 2.7 copy-start.16
  389.8 3.0 copy-start.15
  392.8 55.2 %copy-start.5 = (f32[4,256,256]{2,1,0:T(8,128)S(1)}, f32[4,256,256]{2,1,0:T(8,128)}, u32[]{:S(2)}) copy-start(f32[4,256,256]{2,1,0:T(8,128)} %param.8) | copy-start | bytes 3145732
  392.8 57.6 %copy-start.1 = (f32[6,3,31]{2,1,0:T(4,128)S(1)}, f32[6,3,31]{2,1,0:T(4,128)}, u32[]{:S(2)}) copy-start(f32[6,3,31]{2,1,0:T(4,128)} %param.13) | copy-start | bytes 6700
Sparse Core Ops, SparseCore 0:
  396.6 51.3 all-reduce.1
where the time goes:
time: 463 us; the launch traced here: 458 us
  waiting for transfers between devices  286 us (62%)
  local copies, waits for them, and re-layouts  56 us (12%)
  matrix products  53.1 us (11%)
  starting transfers between devices  35.2 us (8%)
  between operations  20.2 us (4%)
  other arithmetic  7.42 us (2%)
    all_to_all x2, waiting for transfers between devices, shards(): lax.all_to_all(adjoint, 'blk', split_axis=1, concat_axis=2, tiled=True)  117 us
    all_to_all x2, waiting for transfers between devices, shards(): lax.all_to_all(rank_terms, 'blk', split_axis=2, concat_axis=1, tiled=True)  105 us
    psum x1, waiting for transfers between devices, shards(): summed_logs = lax.psum(log_mean, 'grp')  51.5 us
    dot_general x6, matrix products, banded(): jnp.einsum('imt,rt->rim', onehot, taps, precision=lax.Precision.HIGHEST)  15.8 us
    all_to_all x2, waiting for transfers between devices, shards(): lax.all_to_all(outgoing[0], 'blk', split_axis=0, concat_axis=0, tiled=True)  9.69 us
    all_to_all x2, starting transfers between devices, shards(): lax.all_to_all(outgoing[1], 'blk', split_axis=0, concat_axis=0, tiled=True)  9.69 us
    scatter x2, local copies, waits for them, and re-layouts, shards(): observed = jnp.zeros((planes_all, strip_rows, col_count), jnp.bfloat16).a...  9.66 us
  transfers between devices with their start and end apart: 9, of which 9 were waited for; matrix products, arithmetic and copies ran while one was open for 20% of the time, Pallas kernels for 0%

commit v1 on v0

v1 whole, which is shorter than its diff:
```python
import jax
import jax.numpy as jnp
from jax import lax
from jax.sharding import PartitionSpec as P

VSLOT = 2
HIGH = lax.Precision.HIGH


def band(taps, rows, cols, lead):
    width = taps.shape[-1]
    shift = lax.broadcasted_iota(jnp.int32, (rows, cols), 1) - lax.broadcasted_iota(
        jnp.int32, (rows, cols), 0
    )
    shift = shift - lead + width // 2
    out = jnp.zeros(taps.shape[:-1] + (rows, cols), jnp.float32)
    for t in range(width):
        out = jnp.where(shift == t, taps[..., t, None, None], out)
    return out


def shards(estimate, measured, tile_plane, tile_strip, view_group, kernel_cols, kernel_rows, kernel_planes):
    cz, ny, nx = estimate.shape
    blocks = lax.axis_size("blk")
    groups = lax.axis_size("grp")
    nz = cz * blocks
    py = ny // blocks
    half = kernel_rows.shape[-1] // 2
    lead = -(-half // 8) * 8
    ext = py + 2 * lead
    tiles = measured.shape[1]
    per = tiles // blocks

    matches = (view_group == lax.axis_index("grp")).astype(jnp.int32)
    ranking = jnp.cumsum(matches) - matches
    members = jnp.sum(matches).astype(jnp.float32)
    ids = jnp.arange(view_group.shape[0], dtype=jnp.int32)
    picked = [matches * (ranking == s).astype(jnp.int32) for s in range(VSLOT)]
    chosen = [jnp.sum(p * ids) for p in picked]
    weights = jnp.stack([jnp.sum(p).astype(jnp.float32) / members for p in picked])

    padded = jnp.pad(estimate, ((0, 0), (lead, lead), (0, 0)))
    windows = jnp.stack([padded[:, j * py : j * py + ext] for j in range(blocks)])
    pencil = lax.all_to_all(windows, "blk", 0, 0, tiled=True).reshape(nz, ext, nx)

    pick = lambda a: jnp.stack([lax.dynamic_index_in_dim(a, c, 0, keepdims=False) for c in chosen])
    pieces, planes, strips = pick(measured), pick(tile_plane), pick(tile_strip)
    hits = (strips[:, :, None] == jnp.arange(blocks, dtype=jnp.int32)).astype(jnp.int32)
    before = jnp.cumsum(hits, axis=1) - hits
    positions = strips * per + jnp.sum(before * hits, axis=2)
    order = positions[:, None, :] == jnp.arange(tiles, dtype=jnp.int32)[None, :, None]
    send_planes = jnp.sum(jnp.where(order, planes[:, None, :], 0), axis=2)
    send = jnp.einsum("vpi,viyx->pvyx", order.astype(jnp.bfloat16), pieces)
    got = lax.all_to_all(send, "blk", 0, 0, tiled=True)
    got_planes = lax.all_to_all(send_planes.T, "blk", 0, 0, tiled=True)
    place = (got_planes[None] == jnp.arange(nz, dtype=jnp.int32)[:, None, None]).astype(jnp.bfloat16)
    observed = jnp.einsum("ptv,tvyx->vpyx", place, got).astype(jnp.float32)

    kc, kr, kp = pick(kernel_cols), pick(kernel_rows), pick(kernel_planes)
    bx = band(kc, nx, nx, 0)
    by = band(kr, py, ext, lead)
    bz = band(kp, nz, nz, 0)
    byw = by * weights[:, None, None, None]

    t = jnp.einsum("zmx,vrim->vrzix", pencil, by, precision=HIGH)
    t = jnp.einsum("vrzix,vrnx->vrzin", t, bx, precision=HIGH)
    blurred = jnp.einsum("vrzin,vrpz->vpin", t, bz, precision=HIGH)
    ratios = observed / blurred
    a = jnp.einsum("vpin,vrpz->vrzin", ratios, bz, precision=HIGH)
    a = jnp.einsum("vrzin,vrnx->vrzix", a, bx, precision=HIGH)
    wide = jnp.einsum("vrzix,vrim->zmx", a, byw, precision=HIGH)

    chunk = min(py, lead)
    average = wide[:, lead : lead + py]
    for d in range(1, lead // chunk + 1):
        up = wide[:, lead + py + (d - 1) * chunk : lead + py + d * chunk]
        down = wide[:, lead - d * chunk : lead - (d - 1) * chunk]
        up = lax.ppermute(up, "blk", [(i, i + d) for i in range(blocks - d)])
        down = lax.ppermute(down, "blk", [(i, i - d) for i in range(d, blocks)])
        rest = py - chunk
        average = average + jnp.pad(up, ((0, 0), (0, rest), (0, 0))) + jnp.pad(down, ((0, 0), (rest, 0), (0, 0)))
    logs = jnp.log(average)
    logs = lax.all_to_all(logs.reshape(blocks, cz, py, nx), "blk", 0, 0, tiled=True)
    summed = lax.psum(logs, "grp")
    summed = jnp.transpose(summed, (1, 0, 2, 3)).reshape(cz, ny, nx)
    return estimate * jnp.exp(summed / groups)


def solution(mesh):
    in_specs = (
        P("blk", None, None),
        P(None, "blk", None, None),
        P(None, "blk"),
        P(None, "blk"),
        P(),
        P(),
        P(),
        P(),
    )
    return jax.shard_map(
        shards, mesh=mesh, in_specs=in_specs, out_specs=P("blk", None, None), check_vma=False
    )
```

time: 463 us -> 316 us (0.68)
  waiting for transfers between devices: 286 us -> 108 us
  blocking collectives: 0 us -> 36.4 us
  other arithmetic: 7.42 us -> 28.5 us
  starting transfers between devices: 35.2 us -> 18 us
  matrix products: 53.1 us -> 39.1 us
    all_to_all x8 -> x3, waiting for transfers between devices: 234 us -> 53.7 us  [the longest x1 33 us: shards(): lax.all_to_all(windows, 'blk', 0, 0, tiled=True).reshape(nz, ext, nx)]
    broadcast_in_dim x0 -> x62, local copies, waits for them, and re-layouts: none -> 42.3 us  [band(): out = jnp.where(shift == t, taps[..., t, None, None], out)]
    all_to_all x0 -> x1, blocking collectives: none -> 36.4 us  [shards(): lax.all_to_all(logs.reshape(blocks, cz, py, nx), 'blk', 0, 0, tiled=True)]
    all_to_all x8 -> x3, starting transfers between devices: 34.9 us -> 15.1 us  [the longest x1 6.35 us: shards(): got_planes = lax.all_to_all(send_planes.T, 'blk', 0, 0, tiled=True)]
    scatter x6 -> x0, local copies, waits for them, and re-layouts: 19.7 us -> none  [the longest x2 9.66 us: shards(): observed = jnp.zeros((planes_all, strip_rows, col_count), jnp.bfloat16).a...]
    eq x0 -> x48, other arithmetic: none -> 18.7 us  [band(): out = jnp.where(shift == t, taps[..., t, None, None], out)]
    dot_general x18 -> x8, matrix products: 53.1 us -> 39.1 us  [the longest x1 11 us: shards(): a = jnp.einsum('vrzin,vrnx->vrzix', a, bx, precision=HIGH)]
    dot_general x4 -> x0, local copies, waits for them, and re-layouts: 9.46 us -> none  [the longest x2 7.05 us: shards(): jnp.einsum('iyx,rim->rmyx', ratios, band_planes, precision=highest)]
  transfers between devices with their start and end apart: 9 -> 6, of which waited for: 9 -> 5; matrix products, arithmetic and copies ran while one was open for 20% -> 26% of each run, Pallas kernels for 0% -> 0%
where the time goes in v1:
time: 316 us; the launch traced here: 311 us
  waiting for transfers between devices  108 us (34%)
  local copies, waits for them, and re-layouts  59.3 us (19%)
  matrix products  39.1 us (12%)
  blocking collectives  36.4 us (12%)
  other arithmetic  28.5 us (9%)
  between operations  21.8 us (7%)
  starting transfers between devices  18 us (6%)
    psum x1, waiting for transfers between devices, shards(): summed = lax.psum(logs, 'grp')  51.6 us
    broadcast_in_dim x62, local copies, waits for them, and re-layouts, band(): out = jnp.where(shift == t, taps[..., t, None, None], out)  42.3 us
    all_to_all x1, blocking collectives, shards(): lax.all_to_all(logs.reshape(blocks, cz, py, nx), 'blk', 0, 0, tiled=True)  36.4 us
    all_to_all x1, waiting for transfers between devices, shards(): lax.all_to_all(windows, 'blk', 0, 0, tiled=True).reshape(nz, ext, nx)  33 us
    all_to_all x1, waiting for transfers between devices, shards(): got = lax.all_to_all(send, 'blk', 0, 0, tiled=True)  20.7 us
    eq x48, other arithmetic, band(): out = jnp.where(shift == t, taps[..., t, None, None], out)  18.7 us
    dot_general x1, matrix products, shards(): a = jnp.einsum('vrzin,vrnx->vrzix', a, bx, precision=HIGH)  11 us
    dot_general x1, matrix products, shards(): t = jnp.einsum('vrzix,vrnx->vrzin', t, bx, precision=HIGH)  10.8 us
  transfers between devices with their start and end apart: 6, of which 5 were waited for; matrix products, arithmetic and copies ran while one was open for 26% of the time, Pallas kernels for 0%

profile of v1, /device:TPU:0, one launch (start us, length us, event | category | flops | bytes accessed | tf_op | source)
XLA Modules:
  0.0 310.9 jit_solution(15629209679689618100)
XLA Ops:
  7.4 1.4 fusion.249
  12.8 0.8 constant_dynamic-slice_fusion.7
  13.5 0.8 constant_dynamic-slice_fusion.5
  15.5 6.4 %all-to-all-start = ((s32[8,4,2]{1,2,0:T(2,128)}), s32[8,4,2]{1,2,0:T(2,128)S(1)}, u32[]{:S(2)}, u32[]{:S(2)}) async-start(s32[8,4,2]{1,2,0:T(2,128)} %copy.106), calls=%async_computation | async-start | bytes 16384 | tf_op jit(solution)/shard_map/all_to_all | solution.py:55
  31.4 0.7 constant_dynamic-slice_fusion.1
  32.4 0.8 fusion.160
  33.2 0.8 fusion.178
  34.0 0.8 fusion.196
  34.7 0.8 fusion.214
  77.9 1.3 constant_dynamic-slice_fusion.3
  80.2 1.6 copy.110
  84.4 5.1 %all-to-all-start.1 = ((bf16[32,2,32,256]{3,2,1,0:T(8,128)(2,1)}), bf16[32,2,32,256]{3,2,1,0:T(8,128)(2,1)S(1)}, u32[]{:S(2)}, u32[]{:S(2)}) async-start(bf16[32,2,32,256]{3,2,1,0:T(8,128)(2,1)} %copy.110), calls=%async_computation.1 | async-start | bytes 2097152 | tf_op jit(solution)/shard_map/all_to_all | solution.py:54
  89.6 0.7 fusion.17
  90.3 0.7 bitcast_dynamic-update-slice_fusion.5
  91.0 0.7 bitcast_dynamic-update-slice_fusion.4
  91.8 0.7 bitcast_dynamic-update-slice_fusion.3
  92.5 0.7 bitcast_dynamic-update-slice_fusion.2
  93.2 0.7 bitcast_dynamic-update-slice_fusion.1
  93.9 0.7 bitcast_dynamic-update-slice_fusion
  94.6 0.7 fusion.19
  95.4 20.7 %all-to-all-done.1 = bf16[32,2,32,256]{3,2,1,0:T(8,128)(2,1)S(1)} async-done(((bf16[32,2,32,256]{3,2,1,0:T(8,128)(2,1)}), bf16[32,2,32,256]{3,2,1,0:T(8,128)(2,1)S(1)}, u32[]{:S(2)}, u32[]{:S(2)}) %all-to-all-start.1) | async-done | bytes 1048608 | tf_op jit(solution)/shard_map/all_to_all | solution.py:54
  116.1 1.0 copy-done.2
  117.1 3.6 %all-to-all-start.2 = ((f32[8,4,64,256]{3,2,1,0:T(8,128)}), f32[8,4,64,256]{3,2,1,0:T(8,128)S(1)}, u32[]{:S(2)}, u32[]{:S(2)}) async-start(f32[8,4,64,256]{3,2,1,0:T(8,128)} %fusion.19), calls=%async_computation.2 | async-start | bytes 4194304 | tf_op jit(solution)/shard_map/all_to_all | solution.py:44
  123.9 0.7 fusion.28
  124.7 0.7 fusion.30
  125.4 0.7 fusion.32
  126.8 0.7 fusion.36
  127.5 0.7 fusion.38
  128.2 0.7 fusion.40
  128.9 0.7 fusion.42
  130.4 0.7 fusion.46
  131.1 0.7 fusion.48
  132.4 1.4 eq.730
  133.7 2.9 fusion.14
  136.7 33.0 %all-to-all-done.2 = f32[8,4,64,256]{3,2,1,0:T(8,128)S(1)} async-done(((f32[8,4,64,256]{3,2,1,0:T(8,128)}), f32[8,4,64,256]{3,2,1,0:T(8,128)S(1)}, u32[]{:S(2)}, u32[]{:S(2)}) %all-to-all-start.2) | async-done | bytes 2097184 | tf_op jit(solution)/shard_map/all_to_all | solution.py:44
  169.9 4.2 %convolution_bitcast_fusion = f32[2,3,32,32,256]{4,3,2,1,0:T(8,128)S(1)} fusion(f32[32,64,256,1,1]{2,1,0,4,3:T(8,128)S(1)} %bitcast.177, f32[2,3]{0,1:T(4,128)} %bitcast.239, pred[32,64]{1,0:T(8,128)(4,1)S(1)} %get-tuple-element.121, f32[2,3]{0,1:T(4,128)} %bitcast.237, pred[32,64]{1,0:T(8,128)(4,1)S(1)} %get-tuple-element.122, f32[2,3]{0,1:T(4,128)} %bitcast.235, ...), kind=kOutput, calls=%fused_computation.4 | convolution fusion | flops 604360704 | bytes 8452840 | tf_op jit(solution)/shard_map/zmx,vrim->vrzix/dot_general | solution.py:65
  174.5 10.8 %fusion.2 = f32[2,3,32,32,256]{4,2,1,3,0:T(8,128)S(1)} fusion(f32[2,3,32,32,256]{4,3,2,1,0:T(8,128)S(1)} %convolution_bitcast_fusion, f32[2,3]{0,1:T(4,128)} %bitcast.302, pred[256,256]{1,0:T(8,128)(4,1)S(1)} %get-tuple-element.151, f32[2,3]{0,1:T(4,128)} %bitcast.300, pred[256,256]{1,0:T(8,128)(4,1)S(1)} %get-tuple-element.152, f32[2,3]{0,1:T(4,128)} %bitcast.298, ...), kind=kOutput, calls=%fused_computation.2 | convolution fusion | flops 2428108800 | bytes 14615272 | tf_op jit(solution)/shard_map/vrzix,vrnx->vrzin/dot_general | solution.py:66
  185.6 3.2 %fusion.51 = f32[2,32,32,256,1]{3,1,4,2,0:T(8,128)S(1)} fusion(f32[2,3,32,32,256]{4,2,1,3,0:T(8,128)S(1)} %fusion.2, f32[2,3]{1,0:T(2,128)} %get-tuple-element.34, f32[2,3]{1,0:T(2,128)} %get-tuple-element.35, f32[2,3]{1,0:T(2,128)} %get-tuple-element.33, f32[2,3]{1,0:T(2,128)} %get-tuple-element.32, f32[2,3]{1,0:T(2,128)} %get-tuple-element.31, ...), kind=kOutput, calls=%fused_computation.68 | convolution fusion | flops 302180352 | bytes 8421096 | tf_op jit(solution)/shard_map/vrzin,vrpz->vpin/dot_general | solution.py:67
  189.1 2.9 fusion.4
  192.4 11.0 %fusion = f32[2,3,32,32,256]{4,3,0,2,1:T(8,128)S(1)} fusion(f32[2,3,32,32,256]{4,2,3,1,0:T(8,128)S(1)} %fusion.4, f32[2,3]{0,1:T(4,128)} %bitcast.303, f32[2,3]{0,1:T(4,128)} %bitcast.301, f32[2,3]{0,1:T(4,128)} %bitcast.299, f32[2,3]{0,1:T(4,128)} %bitcast.297, f32[2,3]{0,1:T(4,128)} %bitcast.295, f32[2,3]{0,1:T(4,128)} %bitcast.293, f32[2,3]{0,1:T(4,128)} %bitcast.291, ...), kind=kOutput, calls=%fused_computation | convolution fusion | flops 2428108800 | bytes 14615272 | tf_op jit(solution)/shard_map/vrzin,vrnx->vrzix/dot_general | solution.py:70
  203.8 3.6 %convolution_bitcast_fusion.1 = f32[32,64,256]{2,1,0:T(8,128)S(1)} fusion(f32[2,3,32,32,256]{4,3,0,2,1:T(8,128)S(1)} %fusion, f32[2]{0:T(128)} %pad_maximum_fusion.3, f32[2,3]{0,1:T(4,128)} %bitcast.240, f32[2,3]{0,1:T(4,128)} %bitcast.238, f32[2,3]{0,1:T(4,128)} %bitcast.236, f32[2,3]{0,1:T(4,128)} %bitcast.234, f32[2,3]{0,1:T(4,128)} %bitcast.218, ...), kind=kOutput, calls=%fused_computation.9 | convolution fusion | flops 604372992 | bytes 8452848 | tf_op jit(solution)/shard_map/vrzix,vrim->zmx/dot_general | solution.py:71
  207.5 1.5 collective-permute-start
  209.0 1.3 collective-permute-start.1
  210.5 2.3 collective-permute-done.1
  213.1 36.4 %all_to_all.24 = f32[8,4,32,256]{3,2,1,0:T(8,128)} all-to-all(f32[8,4,32,256]{3,2,1,0:T(8,128)S(1)} %bitcast.178), channel_id=1, replica_groups=mesh['grp'=4,'blk'=8] {'blk'}, dimensions={0} | all-to-all | bytes 2097152 | tf_op jit(solution)/shard_map/all_to_all | solution.py:83
  249.5 51.6 %all-reduce.5.cloned.1.call-done = f32[8,4,32,256]{3,2,1,0:T(8,128)} async-done(((f32[8,4,32,256]{3,2,1,0:T(8,128)}), f32[8,4,32,256]{3,2,1,0:T(8,128)}) %all-reduce.5.cloned.1.call-update) | async-done | bytes 1048592 | tf_op jit(solution)/shard_map/psum | solution.py:84
  301.1 1.4 exponential_bitcast_fusion
  302.5 1.1 bitcast_multiply_fusion
  (337 shorter events, 62.0 us)
Async XLA Ops:
  15.5 68.4 %all-to-all-start = ((s32[8,4,2]{1,2,0:T(2,128)}), s32[8,4,2]{1,2,0:T(2,128)S(1)}, u32[]{:S(2)}, u32[]{:S(2)}) async-start(s32[8,4,2]{1,2,0:T(2,128)} %copy.106), calls=%async_computation | async-start | bytes 16384 | tf_op jit(solution)/shard_map/all_to_all | solution.py:55
  84.4 31.7 %all-to-all-start.1 = ((bf16[32,2,32,256]{3,2,1,0:T(8,128)(2,1)}), bf16[32,2,32,256]{3,2,1,0:T(8,128)(2,1)S(1)}, u32[]{:S(2)}, u32[]{:S(2)}) async-start(bf16[32,2,32,256]{3,2,1,0:T(8,128)(2,1)} %copy.110), calls=%async_computation.1 | async-start | bytes 2097152 | tf_op jit(solution)/shard_map/all_to_all | solution.py:54
  117.1 52.6 %all-to-all-start.2 = ((f32[8,4,64,256]{3,2,1,0:T(8,128)}), f32[8,4,64,256]{3,2,1,0:T(8,128)S(1)}, u32[]{:S(2)}, u32[]{:S(2)}) async-start(f32[8,4,64,256]{3,2,1,0:T(8,128)} %fusion.19), calls=%async_computation.2 | async-start | bytes 4194304 | tf_op jit(solution)/shard_map/all_to_all | solution.py:44
  120.7 180.4 %all-reduce.5.cloned.1.call-start = ((), (), s32[]{:S(2)}) async-start(), calls=%async_computation.4 | async-start | bytes 2097152 | tf_op jit(solution)/shard_map/psum | solution.py:84
  174.4 10.9 %copy-start.71 = (f32[2,3]{1,0:T(2,128)S(1)}, f32[2,3]{1,0:T(2,128)}, u32[]{:S(2)}) copy-start(f32[2,3]{1,0:T(2,128)} %get-tuple-element.5) | copy-start | bytes 76
  174.4 10.9 %copy-start.72 = (f32[2,3]{1,0:T(2,128)S(1)}, f32[2,3]{1,0:T(2,128)}, u32[]{:S(2)}) copy-start(f32[2,3]{1,0:T(2,128)} %get-tuple-element.6) | copy-start | bytes 76
  174.4 10.9 %copy-start.73 = (f32[2,3]{1,0:T(2,128)S(1)}, f32[2,3]{1,0:T(2,128)}, u32[]{:S(2)}) copy-start(f32[2,3]{1,0:T(2,128)} %get-tuple-element.7) | copy-start | bytes 76
  192.0 11.4 %copy-start.30 = (pred[32,64]{1,0:T(8,128)(4,1)S(1)}, pred[32,64]{1,0:T(8,128)(4,1)}, u32[]{:S(2)}) copy-start(pred[32,64]{1,0:T(8,128)(4,1)} %get-tuple-element.126) | copy-start | bytes 6148
  192.0 11.4 %copy-start.31 = (pred[32,64]{1,0:T(8,128)(4,1)S(1)}, pred[32,64]{1,0:T(8,128)(4,1)}, u32[]{:S(2)}) copy-start(pred[32,64]{1,0:T(8,128)(4,1)} %get-tuple-element.127) | copy-start | bytes 6148
  192.0 11.4 %copy-start.32 = (pred[32,64]{1,0:T(8,128)(4,1)S(1)}, pred[32,64]{1,0:T(8,128)(4,1)}, u32[]{:S(2)}) copy-start(pred[32,64]{1,0:T(8,128)(4,1)} %get-tuple-element.128) | copy-start | bytes 6148
  192.0 11.4 %copy-start.33 = (pred[32,64]{1,0:T(8,128)(4,1)S(1)}, pred[32,64]{1,0:T(8,128)(4,1)}, u32[]{:S(2)}) copy-start(pred[32,64]{1,0:T(8,128)(4,1)} %get-tuple-element.129) | copy-start | bytes 6148
  192.0 11.4 %copy-start.34 = (pred[32,64]{1,0:T(8,128)(4,1)S(1)}, pred[32,64]{1,0:T(8,128)(4,1)}, u32[]{:S(2)}) copy-start(pred[32,64]{1,0:T(8,128)(4,1)} %get-tuple-element.130) | copy-start | bytes 6148
  192.1 11.4 %copy-start.35 = (pred[32,64]{1,0:T(8,128)(4,1)S(1)}, pred[32,64]{1,0:T(8,128)(4,1)}, u32[]{:S(2)}) copy-start(pred[32,64]{1,0:T(8,128)(4,1)} %get-tuple-element.131) | copy-start | bytes 6148
  192.1 11.4 %copy-start.36 = (pred[32,64]{1,0:T(8,128)(4,1)S(1)}, pred[32,64]{1,0:T(8,128)(4,1)}, u32[]{:S(2)}) copy-start(pred[32,64]{1,0:T(8,128)(4,1)} %get-tuple-element.132) | copy-start | bytes 6148
  192.1 11.4 %copy-start.37 = (pred[32,64]{1,0:T(8,128)(4,1)S(1)}, pred[32,64]{1,0:T(8,128)(4,1)}, u32[]{:S(2)}) copy-start(pred[32,64]{1,0:T(8,128)(4,1)} %get-tuple-element.133) | copy-start | bytes 6148
  192.1 11.4 %copy-start.38 = (pred[32,64]{1,0:T(8,128)(4,1)S(1)}, pred[32,64]{1,0:T(8,128)(4,1)}, u32[]{:S(2)}) copy-start(pred[32,64]{1,0:T(8,128)(4,1)} %get-tuple-element.134) | copy-start | bytes 6148
  192.1 11.4 %copy-start.39 = (pred[32,64]{1,0:T(8,128)(4,1)S(1)}, pred[32,64]{1,0:T(8,128)(4,1)}, u32[]{:S(2)}) copy-start(pred[32,64]{1,0:T(8,128)(4,1)} %get-tuple-element.135) | copy-start | bytes 6148
  192.1 11.4 %copy-start.40 = (pred[32,64]{1,0:T(8,128)(4,1)S(1)}, pred[32,64]{1,0:T(8,128)(4,1)}, u32[]{:S(2)}) copy-start(pred[32,64]{1,0:T(8,128)(4,1)} %get-tuple-element.136) | copy-start | bytes 6148
  192.1 11.4 %copy-start.41 = (pred[32,64]{1,0:T(8,128)(4,1)S(1)}, pred[32,64]{1,0:T(8,128)(4,1)}, u32[]{:S(2)}) copy-start(pred[32,64]{1,0:T(8,128)(4,1)} %get-tuple-element.137) | copy-start | bytes 6148
  192.1 11.4 %copy-start.42 = (pred[32,64]{1,0:T(8,128)(4,1)S(1)}, pred[32,64]{1,0:T(8,128)(4,1)}, u32[]{:S(2)}) copy-start(pred[32,64]{1,0:T(8,128)(4,1)} %get-tuple-element.138) | copy-start | bytes 6148
  192.1 11.4 %copy-start.43 = (pred[32,64]{1,0:T(8,128)(4,1)S(1)}, pred[32,64]{1,0:T(8,128)(4,1)}, u32[]{:S(2)}) copy-start(pred[32,64]{1,0:T(8,128)(4,1)} %get-tuple-element.139) | copy-start | bytes 6148
  192.1 11.4 %copy-start.44 = (pred[32,64]{1,0:T(8,128)(4,1)S(1)}, pred[32,64]{1,0:T(8,128)(4,1)}, u32[]{:S(2)}) copy-start(pred[32,64]{1,0:T(8,128)(4,1)} %get-tuple-element.140) | copy-start | bytes 6148
  192.2 11.4 %copy-start.45 = (pred[32,64]{1,0:T(8,128)(4,1)S(1)}, pred[32,64]{1,0:T(8,128)(4,1)}, u32[]{:S(2)}) copy-start(pred[32,64]{1,0:T(8,128)(4,1)} %get-tuple-element.141) | copy-start | bytes 6148
  192.2 11.4 %copy-start.46 = (pred[32,64]{1,0:T(8,128)(4,1)S(1)}, pred[32,64]{1,0:T(8,128)(4,1)}, u32[]{:S(2)}) copy-start(pred[32,64]{1,0:T(8,128)(4,1)} %get-tuple-element.142) | copy-start | bytes 6148
  192.2 11.4 %copy-start.47 = (pred[32,64]{1,0:T(8,128)(4,1)S(1)}, pred[32,64]{1,0:T(8,128)(4,1)}, u32[]{:S(2)}) copy-start(pred[32,64]{1,0:T(8,128)(4,1)} %get-tuple-element.143) | copy-start | bytes 6148
  192.2 11.4 %copy-start.48 = (pred[32,64]{1,0:T(8,128)(4,1)S(1)}, pred[32,64]{1,0:T(8,128)(4,1)}, u32[]{:S(2)}) copy-start(pred[32,64]{1,0:T(8,128)(4,1)} %get-tuple-element.144) | copy-start | bytes 6148
  192.2 11.4 %copy-start.49 = (pred[32,64]{1,0:T(8,128)(4,1)S(1)}, pred[32,64]{1,0:T(8,128)(4,1)}, u32[]{:S(2)}) copy-start(pred[32,64]{1,0:T(8,128)(4,1)} %get-tuple-element.145) | copy-start | bytes 6148
  192.2 11.4 %copy-start.50 = (pred[32,64]{1,0:T(8,128)(4,1)S(1)}, pred[32,64]{1,0:T(8,128)(4,1)}, u32[]{:S(2)}) copy-start(pred[32,64]{1,0:T(8,128)(4,1)} %get-tuple-element.146) | copy-start | bytes 6148
  192.2 11.4 %copy-start.51 = (pred[32,64]{1,0:T(8,128)(4,1)S(1)}, pred[32,64]{1,0:T(8,128)(4,1)}, u32[]{:S(2)}) copy-start(pred[32,64]{1,0:T(8,128)(4,1)} %get-tuple-element.147) | copy-start | bytes 6148
  192.2 11.4 %copy-start.52 = (pred[32,64]{1,0:T(8,128)(4,1)S(1)}, pred[32,64]{1,0:T(8,128)(4,1)}, u32[]{:S(2)}) copy-start(pred[32,64]{1,0:T(8,128)(4,1)} %get-tuple-element.148) | copy-start | bytes 6148
  192.2 11.4 %copy-start.53 = (pred[32,64]{1,0:T(8,128)(4,1)S(1)}, pred[32,64]{1,0:T(8,128)(4,1)}, u32[]{:S(2)}) copy-start(pred[32,64]{1,0:T(8,128)(4,1)} %get-tuple-element.149) | copy-start | bytes 6148
  192.2 11.4 %copy-start.54 = (pred[32,64]{1,0:T(8,128)(4,1)S(1)}, pred[32,64]{1,0:T(8,128)(4,1)}, u32[]{:S(2)}) copy-start(pred[32,64]{1,0:T(8,128)(4,1)} %get-tuple-element.150) | copy-start | bytes 6148
  192.3 11.4 %copy-start.55 = (pred[32,64]{1,0:T(8,128)(4,1)S(1)}, pred[32,64]{1,0:T(8,128)(4,1)}, u32[]{:S(2)}) copy-start(pred[32,64]{1,0:T(8,128)(4,1)} %fusion.126) | copy-start | bytes 6148
  192.3 11.4 %copy-start.58 = (f32[2,3,1]{0,1,2:T(4,128)S(1)}, f32[2,3,1]{0,1,2:T(4,128)}, u32[]{:S(2)}) copy-start(f32[2,3,1]{0,1,2:T(4,128)} %copy.174) | copy-start | bytes 76
  192.3 11.4 %copy-start.59 = (f32[2,3,1]{0,1,2:T(4,128)S(1)}, f32[2,3,1]{0,1,2:T(4,128)}, u32[]{:S(2)}) copy-start(f32[2,3,1]{0,1,2:T(4,128)} %copy.175) | copy-start | bytes 76
  192.3 11.4 %copy-start.60 = (f32[2,3,1]{0,1,2:T(4,128)S(1)}, f32[2,3,1]{0,1,2:T(4,128)}, u32[]{:S(2)}) copy-start(f32[2,3,1]{0,1,2:T(4,128)} %copy.176) | copy-start | bytes 76
  192.3 11.4 %copy-start.61 = (f32[2,3,1]{0,1,2:T(4,128)S(1)}, f32[2,3,1]{0,1,2:T(4,128)}, u32[]{:S(2)}) copy-start(f32[2,3,1]{0,1,2:T(4,128)} %copy.177) | copy-start | bytes 76
  192.3 11.4 %copy-start.62 = (f32[2,3,1]{0,1,2:T(4,128)S(1)}, f32[2,3,1]{0,1,2:T(4,128)}, u32[]{:S(2)}) copy-start(f32[2,3,1]{0,1,2:T(4,128)} %copy.178) | copy-start | bytes 76
  192.3 11.4 %copy-start.63 = (f32[2,3,1]{0,1,2:T(4,128)S(1)}, f32[2,3,1]{0,1,2:T(4,128)}, u32[]{:S(2)}) copy-start(f32[2,3,1]{0,1,2:T(4,128)} %copy.179) | copy-start | bytes 76
  192.3 11.4 %copy-start.64 = (f32[2,3,1]{0,1,2:T(4,128)S(1)}, f32[2,3,1]{0,1,2:T(4,128)}, u32[]{:S(2)}) copy-start(f32[2,3,1]{0,1,2:T(4,128)} %copy.180) | copy-start | bytes 76
  192.3 11.4 %copy-start.65 = (f32[2,3,1]{0,1,2:T(4,128)S(1)}, f32[2,3,1]{0,1,2:T(4,128)}, u32[]{:S(2)}) copy-start(f32[2,3,1]{0,1,2:T(4,128)} %copy.181) | copy-start | bytes 76
  192.3 11.4 %copy-start.66 = (f32[2,3,1]{0,1,2:T(4,128)S(1)}, f32[2,3,1]{0,1,2:T(4,128)}, u32[]{:S(2)}) copy-start(f32[2,3,1]{0,1,2:T(4,128)} %copy.182) | copy-start | bytes 76
  192.4 11.4 %copy-start.67 = (f32[2,3,1]{0,1,2:T(4,128)S(1)}, f32[2,3,1]{0,1,2:T(4,128)}, u32[]{:S(2)}) copy-start(f32[2,3,1]{0,1,2:T(4,128)} %copy.183) | copy-start | bytes 76
  192.4 11.4 %copy-start.68 = (f32[2,3,1]{0,1,2:T(4,128)S(1)}, f32[2,3,1]{0,1,2:T(4,128)}, u32[]{:S(2)}) copy-start(f32[2,3,1]{0,1,2:T(4,128)} %copy.166) | copy-start | bytes 76
  192.4 11.4 %copy-start.69 = (f32[2,3,1]{0,1,2:T(4,128)S(1)}, f32[2,3,1]{0,1,2:T(4,128)}, u32[]{:S(2)}) copy-start(f32[2,3,1]{0,1,2:T(4,128)} %copy.184) | copy-start | bytes 76
  192.4 11.4 %copy-start.70 = (f32[2,3,1]{0,1,2:T(4,128)S(1)}, f32[2,3,1]{0,1,2:T(4,128)}, u32[]{:S(2)}) copy-start(f32[2,3,1]{0,1,2:T(4,128)} %copy.185) | copy-start | bytes 76
  207.5 3.0 collective-permute-start
  209.0 3.8 %collective-permute-start.1 = (f32[32,16,256]{2,1,0:T(8,128)S(1)}, f32[32,16,256]{2,1,0:T(8,128)S(1)}, u32[]{:S(2)}, u32[]{:S(2)}) collective-permute-start(f32[32,16,256]{2,1,0:T(8,128)S(1)} %get-tuple-element.44), channel_id=1, source_target_pairs={{1,0},{2,1},{3,2},{4,3},{5,4},{6,5},{7,6},{9,8},{10,9},{11,10},{12... | collective-permute-start | bytes 1572872 | tf_op jit(solution)/shard_map/ppermute | solution.py:79
  (61 other events, 313.3 us)
Sparse Core Ops, SparseCore 0:
  249.6 51.3 all-reduce.4

commit v2 on v1

--- a/solution.py
+++ b/solution.py
@@ -1,22 +1,154 @@
 import jax
 import jax.numpy as jnp
 from jax import lax
+from jax.experimental import pallas as pl
+from jax.experimental.pallas import tpu as pltpu
 from jax.sharding import PartitionSpec as P
 
 VSLOT = 2
 HIGH = lax.Precision.HIGH
 
 
-def band(taps, rows, cols, lead):
-    width = taps.shape[-1]
-    shift = lax.broadcasted_iota(jnp.int32, (rows, cols), 1) - lax.broadcasted_iota(
-        jnp.int32, (rows, cols), 0
-    )
-    shift = shift - lead + width // 2
-    out = jnp.zeros(taps.shape[:-1] + (rows, cols), jnp.float32)
-    for t in range(width):
-        out = jnp.where(shift == t, taps[..., t, None, None], out)
-    return out
+MESH = pl.DeviceIdType.MESH
+
+
+def band_kernel(*refs):
+    count = len(refs) // 2
+    for row, out in zip(refs[:count], refs[count:]):
+        number, rows, cols = out.shape
+        for n in range(number):
+            wide = jnp.broadcast_to(row[n], (rows, row.shape[-1]))
+            wide = pltpu.roll(wide, 0, 1, stride=1, stride_axis=0)
+            out[n] = wide[:, :cols]
+
+
+def bands(shapes):
+    rows_in, outs = [], []
+    for taps, rows, cols, lead in shapes:
+        number, width = taps.shape
+        half = width // 2
+        span = -(-(max(cols, rows) + lead + width) // 128) * 128
+        row = jnp.pad(taps, ((0, 0), (0, span - width)))
+        row = jnp.roll(row, lead - half, axis=1)
+        rows_in.append(row[:, None, :])
+        outs.append(jax.ShapeDtypeStruct((number, rows, cols), jnp.float32))
+    vmem = pl.BlockSpec(memory_space=pltpu.VMEM)
+    return pl.pallas_call(
+        band_kernel,
+        out_shape=outs,
+        in_specs=[vmem] * len(outs),
+        out_specs=[vmem] * len(outs),
+    )(*rows_in)
+
+
+def finish_kernel(blocks, groups, logs, est, out, got1, send2, got2, s1, r1, s2, r2, s3, r3):
+    me = lax.axis_index("blk")
+    grp = lax.axis_index("grp")
+    cq = est.shape[0] // groups
+    mine = pl.ds(grp * cq, cq)
+    barrier = pltpu.get_barrier_semaphore()
+    for k in range(1, groups):
+        pl.semaphore_signal(barrier, inc=1, device_id=(lax.rem(grp + k, groups), me), device_id_type=MESH)
+    for rel in range(1, blocks):
+        pl.semaphore_signal(barrier, inc=1, device_id=(grp, lax.rem(me + rel, blocks)), device_id_type=MESH)
+    pl.semaphore_wait(barrier, groups + blocks - 2)
+    order = list(range(1, blocks)) + [0]
+
+    first, second, third = {}, {}, {}
+    for rel in order:
+        dest = lax.rem(me + rel, blocks)
+        for k in range(1, groups):
+            peer = lax.rem(grp + k, groups)
+            first[rel, k] = pltpu.make_async_remote_copy(
+                src_ref=logs.at[dest, pl.ds(peer * cq, cq)],
+                dst_ref=got1.at[rel, k - 1],
+                send_sem=s1.at[rel, k - 1],
+                recv_sem=r1.at[rel, k - 1],
+                device_id=(peer, me),
+                device_id_type=MESH,
+            )
+            first[rel, k].start()
+    for rel in order:
+        dest = lax.rem(me + rel, blocks)
+        total = logs[dest, mine]
+        for k in range(1, groups):
+            first[rel, k].wait_recv()
+            total = total + got1[rel, k - 1]
+        if rel == 0:
+            got2[0] = total
+        else:
+            send2[rel] = total
+            second[rel] = pltpu.make_async_remote_copy(
+                src_ref=send2.at[rel],
+                dst_ref=got2.at[rel],
+                send_sem=s2.at[rel],
+                recv_sem=r2.at[rel],
+                device_id=(grp, dest),
+                device_id_type=MESH,
+            )
+            second[rel].start()
+    for rel in order:
+        strip = lax.rem(me + blocks - rel, blocks)
+        if rel != 0:
+            second[rel].wait_recv()
+        out[mine, strip] = est[mine, strip] * jnp.exp(got2[rel] * (1.0 / groups))
+        for k in range(1, groups):
+            third[rel, k] = pltpu.make_async_remote_copy(
+                src_ref=out.at[mine, strip],
+                dst_ref=out.at[mine, strip],
+                send_sem=s3.at[rel, k - 1],
+                recv_sem=r3.at[rel, k - 1],
+                device_id=(lax.rem(grp + k, groups), me),
+                device_id_type=MESH,
+            )
+            third[rel, k].start()
+    for copy in first.values():
+        copy.wait_send()
+    for copy in second.values():
+        copy.wait_send()
+    for copy in third.values():
+        copy.wait_send()
+    for rel in order:
+        strip = lax.rem(me + blocks - rel, blocks)
+        for k in range(1, groups):
+            peer = lax.rem(grp + groups - k, groups)
+            theirs = out.at[pl.ds(peer * cq, cq), strip]
+            pltpu.make_async_remote_copy(
+                src_ref=theirs,
+                dst_ref=theirs,
+                send_sem=s3.at[rel, k - 1],
+                recv_sem=r3.at[rel, k - 1],
+                device_id=(peer, me),
+                device_id_type=MESH,
+            ).wait_recv()
+
+
+def finish(logs, estimate, blocks, groups):
+    cz, ny, nx = estimate.shape
+    py = ny // blocks
+    cq = cz // groups
+    vmem = pl.BlockSpec(memory_space=pltpu.VMEM)
+    dma = pltpu.SemaphoreType.DMA
+    out = pl.pallas_call(
+        lambda *refs: finish_kernel(blocks, groups, *refs),
+        out_shape=jax.ShapeDtypeStruct((cz, blocks, py, nx), jnp.float32),
+        in_specs=[vmem, vmem],
+        out_specs=vmem,
+        scratch_shapes=[
+            pltpu.VMEM((blocks, groups - 1, cq, py, nx), jnp.float32),
+            pltpu.VMEM((blocks, cq, py, nx), jnp.float32),
+            pltpu.VMEM((blocks, cq, py, nx), jnp.float32),
+            dma((blocks, groups - 1)),
+            dma((blocks, groups - 1)),
+            dma((blocks,)),
+            dma((blocks,)),
+            dma((blocks, groups - 1)),
+            dma((blocks, groups - 1)),
+        ],
+        compiler_params=pltpu.CompilerParams(collective_id=0, has_side_effects=True),
+        name="finish",
+    )(logs.reshape(blocks, cz, py, nx), estimate.reshape(cz, blocks, py, nx))
+    return out.reshape(cz, ny, nx)
 
 
 def shards(estimate, measured, tile_plane, tile_strip, view_group, kernel_cols, kernel_rows, kernel_planes):
@@ -57,9 +189,9 @@
     observed = jnp.einsum("ptv,tvyx->vpyx", place, got).astype(jnp.float32)
 
     kc, kr, kp = pick(kernel_cols), pick(kernel_rows), pick(kernel_planes)
-    bx = band(kc, nx, nx, 0)
-    by = band(kr, py, ext, lead)
-    bz = band(kp, nz, nz, 0)
+    flat = lambda k: k.reshape(-1, k.shape[-1])
+    fold = lambda m: m.reshape((VSLOT, -1) + m.shape[1:])
+    bx, by, bz = map(fold, bands([(flat(kc), nx, nx, 0), (flat(kr), py, ext, lead), (flat(kp), nz, nz, 0)]))
     byw = by * weights[:, None, None, None]
 
     t = jnp.einsum("zmx,vrim->vrzix", pencil, by, precision=HIGH)
@@ -80,10 +212,7 @@
         rest = py - chunk
         average = average + jnp.pad(up, ((0, 0), (0, rest), (0, 0))) + jnp.pad(down, ((0, 0), (rest, 0), (0, 0)))
     logs = jnp.log(average)
-    logs = lax.all_to_all(logs.reshape(blocks, cz, py, nx), "blk", 0, 0, tiled=True)
-    summed = lax.psum(logs, "grp")
-    summed = jnp.transpose(summed, (1, 0, 2, 3)).reshape(cz, ny, nx)
-    return estimate * jnp.exp(summed / groups)
+    return finish(logs, estimate, blocks, groups)
 
 
 def solution(mesh):

time: 316 us -> 176 us (0.56); the launches traced: 311 us -> 175 us
  waiting for transfers between devices: 108 us -> 62.6 us
  local copies, waits for them, and re-layouts: 59.3 us -> 18.4 us
  Pallas kernels: 0 us -> 40.2 us
  blocking collectives: 36.4 us -> 0 us
  other arithmetic: 28.5 us -> 4.12 us
  between operations: 21.8 us -> 6.14 us
  matrix products: 39.1 us -> 25.8 us
    psum x1 -> x0, waiting for transfers between devices: 51.6 us -> none  [shards(): summed = lax.psum(logs, 'grp')]
    broadcast_in_dim x62 -> x3, local copies, waits for them, and re-layouts: 42.3 us -> 1.79 us  [bands(): rows_in.append(row[:, None, :])]
    pallas_call x0 -> x2, Pallas kernels: none -> 40.2 us  [the longest x1 37.9 us: finish(): pl.pallas_call(lambda *refs: finish_kernel(blocks, groups, *refs), out_sh...]
    all_to_all x1 -> x0, blocking collectives: 36.4 us -> none  [shards(): lax.all_to_all(logs.reshape(blocks, cz, py, nx), 'blk', 0, 0, tiled=True)]
    eq x48 -> x0, other arithmetic: 18.7 us -> none  [band(): out = jnp.where(shift == t, taps[..., t, None, None], out)]
    all_to_all x1, waiting for transfers between devices: 33 us -> 38.8 us  [shards(): lax.all_to_all(windows, 'blk', 0, 0, tiled=True).reshape(nz, ext, nx)]
    dot_general x1, matrix products: 11 us -> 6.38 us  [shards(): a = jnp.einsum('vrzin,vrnx->vrzix', a, bx, precision=HIGH)]
    dot_general x1, matrix products: 10.8 us -> 6.37 us  [shards(): t = jnp.einsum('vrzix,vrnx->vrzin', t, bx, precision=HIGH)]
  transfers between devices with their start and end apart: 6 -> 5, of which waited for: 5 -> 4; matrix products, arithmetic and copies ran while one was open for 26% -> 9% of each run, Pallas kernels for 0% -> 1%
where the time goes in v2:
time: 176 us; the launch traced here: 175 us
  waiting for transfers between devices  62.6 us (36%)
  Pallas kernels  40.2 us (23%)
  matrix products  25.8 us (15%)
  local copies, waits for them, and re-layouts  18.4 us (10%)
  starting transfers between devices  18.1 us (10%)
  between operations  6.14 us (3%)
  other arithmetic  4.12 us (2%)
    all_to_all x1, waiting for transfers between devices, shards(): lax.all_to_all(windows, 'blk', 0, 0, tiled=True).reshape(nz, ext, nx)  38.8 us
    pallas_call x1, Pallas kernels, finish(): pl.pallas_call(lambda *refs: finish_kernel(blocks, groups, *refs), out_sh...  37.9 us
    all_to_all x1, waiting for transfers between devices, shards(): got = lax.all_to_all(send, 'blk', 0, 0, tiled=True)  20.7 us
    unnamed x20, local copies, waits for them, and re-layouts  8.94 us
    dot_general x1, matrix products, shards(): a = jnp.einsum('vrzin,vrnx->vrzix', a, bx, precision=HIGH)  6.38 us
    dot_general x1, matrix products, shards(): t = jnp.einsum('vrzix,vrnx->vrzin', t, bx, precision=HIGH)  6.37 us
    all_to_all x1, starting transfers between devices, shards(): got_planes = lax.all_to_all(send_planes.T, 'blk', 0, 0, tiled=True)  6.35 us
    dynamic_slice x5, local copies, waits for them, and re-layouts, shards(): lax.dynamic_index_in_dim(a, c, 0, keepdims=False)  4.25 us
  transfers between devices with their start and end apart: 5, of which 4 were waited for; matrix products, arithmetic and copies ran while one was open for 9% of the time, Pallas kernels for 1%

profile of v2, /device:TPU:0, one launch (start us, length us, event | category | flops | bytes accessed | tf_op | source)
XLA Modules:
  0.0 175.4 jit_solution(9641964156029380688)
XLA Ops:
  0.0 0.7 fusion.32
  0.7 0.2 reduce-window.9
  0.8 1.4 fusion.29
  6.3 0.8 constant_dynamic-slice_fusion.5
  7.0 0.8 constant_dynamic-slice_fusion.3
  8.0 0.2 select_reduce_fusion.1
  8.2 0.1 select_reduce_fusion
  8.4 0.6 copy.14
  9.0 6.4 %all-to-all-start = ((s32[8,4,2]{1,2,0:T(2,128)}), s32[8,4,2]{1,2,0:T(2,128)S(1)}, u32[]{:S(2)}, u32[]{:S(2)}) async-start(s32[8,4,2]{1,2,0:T(2,128)} %copy.14), calls=%async_computation | async-start | bytes 16384 | tf_op jit(solution)/shard_map/all_to_all | solution.py:187
  15.3 1.3 constant_dynamic-slice_fusion.1
  16.6 0.3 copy.47
  16.9 0.3 copy.46
  17.2 0.4 convolution_bitcast_fusion.2
  17.6 1.6 copy.18
  19.2 1.7 all-to-all-done
  20.9 3.6 %all-to-all-start.1 = ((bf16[32,2,32,256]{3,2,1,0:T(8,128)(2,1)}), bf16[32,2,32,256]{3,2,1,0:T(8,128)(2,1)S(1)}, u32[]{:S(2)}, u32[]{:S(2)}) async-start(bf16[32,2,32,256]{3,2,1,0:T(8,128)(2,1)} %copy.18), calls=%async_computation.1 | async-start | bytes 2097152 | tf_op jit(solution)/shard_map/all_to_all | solution.py:186
  24.5 0.7 fusion.16
  25.2 0.7 bitcast_dynamic-update-slice_fusion.5
  25.9 0.7 bitcast_dynamic-update-slice_fusion.4
  26.7 0.7 bitcast_dynamic-update-slice_fusion.3
  27.4 0.7 bitcast_dynamic-update-slice_fusion.2
  28.1 0.7 bitcast_dynamic-update-slice_fusion.1
  28.9 0.7 bitcast_dynamic-update-slice_fusion
  29.6 0.7 fusion.18
  30.3 20.7 %all-to-all-done.1 = bf16[32,2,32,256]{3,2,1,0:T(8,128)(2,1)S(1)} async-done(((bf16[32,2,32,256]{3,2,1,0:T(8,128)(2,1)}), bf16[32,2,32,256]{3,2,1,0:T(8,128)(2,1)S(1)}, u32[]{:S(2)}, u32[]{:S(2)}) %all-to-all-start.1) | async-done | bytes 1048608 | tf_op jit(solution)/shard_map/all_to_all | solution.py:186
  51.0 1.0 copy-done.2
  52.0 3.8 %all-to-all-start.2 = ((f32[8,4,64,256]{3,2,1,0:T(8,128)}), f32[8,4,64,256]{3,2,1,0:T(8,128)S(1)}, u32[]{:S(2)}, u32[]{:S(2)}) async-start(f32[8,4,64,256]{3,2,1,0:T(8,128)} %fusion.18), calls=%async_computation.2 | async-start | bytes 4194304 | tf_op jit(solution)/shard_map/all_to_all | solution.py:176
  55.7 0.7 constant_dynamic-slice_fusion.11
  56.6 0.6 broadcast_in_dim.18.refs_0_
  57.2 0.7 constant_dynamic-slice_fusion.7
  58.1 0.6 broadcast_in_dim.30.refs_1_
  58.8 0.6 broadcast_in_dim.31.refs_2_
  61.3 2.3 %shard_map.82 = (f32[6,256,256]{2,1,0:T(8,128)}, f32[6,32,64]{2,1,0:T(8,128)}, f32[6,32,32]{2,1,0:T(8,128)}) custom-call(f32[6,1,384]{2,1,0:T(1,128)} %broadcast_in_dim.18.refs_0_, f32[6,1,128]{2,1,0:T(1,128)} %broadcast_in_dim.30.refs_1_, f32[6,1,128]{2,1,0:T(1,128)} %broadcast_in_dim.31.refs_2_), custom_call_target="tpu_custom_call" | custom-call | tf_op jit(solution)/shard_map/pallas_call | solution.py:36
  63.7 0.1 eq.63
  63.8 1.9 %fusion.13 = bf16[2,32,32,256]{3,1,2,0:T(8,128)(2,1)S(1)} fusion(bf16[32,2,32,256]{3,2,1,0:T(8,128)(2,1)} %copy-done.2, s32[32,2]{0,1:T(2,128)S(1)} %eq.63), kind=kOutput, calls=%fused_computation.20 | convolution fusion | flops 33556480 | bytes 2097408 | tf_op jit(solution)/shard_map/ptv,tvyx->vpyx/dot_general | solution.py:189
  65.8 38.8 %all-to-all-done.2 = f32[8,4,64,256]{3,2,1,0:T(8,128)S(1)} async-done(((f32[8,4,64,256]{3,2,1,0:T(8,128)}), f32[8,4,64,256]{3,2,1,0:T(8,128)S(1)}, u32[]{:S(2)}, u32[]{:S(2)}) %all-to-all-start.2) | async-done | bytes 2097184 | tf_op jit(solution)/shard_map/all_to_all | solution.py:176
  104.5 2.7 %convolution_bitcast_fusion = f32[2,3,32,32,256]{4,3,2,1,0:T(8,128)S(1)} fusion(f32[2,3,32,64,1]{3,2,4,1,0:T(8,128)S(1)} %bitcast.121, f32[32,64,256,1,1]{2,1,0,4,3:T(8,128)S(1)} %bitcast.118), kind=kOutput, calls=%fused_computation.4 | convolution fusion | flops 603979776 | bytes 8437760 | tf_op jit(solution)/shard_map/zmx,vrim->vrzix/dot_general | solution.py:197
  107.2 6.4 %fusion.2 = f32[2,3,32,32,256]{4,2,1,3,0:T(8,128)S(1)} fusion(f32[2,3,256,256,1]{3,2,1,4,0:T(8,128)S(1)} %bitcast.116, f32[2,3,32,32,256]{4,3,2,1,0:T(8,128)S(1)} %convolution_bitcast_fusion), kind=kOutput, calls=%fused_computation.2 | convolution fusion | flops 2415919104 | bytes 14155776 | tf_op jit(solution)/shard_map/vrzix,vrnx->vrzin/dot_general | solution.py:198
  113.6 2.9 %fusion.33 = f32[2,32,32,256,1]{3,1,4,2,0:T(8,128)S(1)} fusion(f32[2,3,32,32,1]{3,2,1,4,0:T(8,128)S(1)} %bitcast.123, f32[2,3,32,32,256]{4,2,1,3,0:T(8,128)S(1)} %fusion.2), kind=kOutput, calls=%fused_computation.80 | convolution fusion | flops 301989888 | bytes 8413184 | tf_op jit(solution)/shard_map/vrzin,vrpz->vpin/dot_general | solution.py:199
  116.5 2.7 %fusion.4 = f32[2,3,32,32,256]{4,2,3,1,0:T(8,128)S(1)} fusion(f32[2,3,32,32,1]{3,2,4,1,0:T(8,128)S(1)} %bitcast.124, f32[2,32,32,256,1]{3,1,4,2,0:T(8,128)S(1)} %fusion.33, bf16[2,32,32,256]{3,1,2,0:T(8,128)(2,1)S(1)} %fusion.13), kind=kOutput, calls=%fused_computation.5 | convolution fusion | flops 303038464 | bytes 9461760 | tf_op jit(solution)/shard_map/vpin,vrpz->vrzin/dot_general | solution.py:201
  119.2 6.4 %fusion = f32[2,3,32,32,256]{4,3,0,2,1:T(8,128)S(1)} fusion(f32[2,3,32,32,256]{4,2,3,1,0:T(8,128)S(1)} %fusion.4, f32[2,3,256,256,1]{3,2,1,0,4:T(8,128)S(1)} %bitcast.117), kind=kOutput, calls=%fused_computation | convolution fusion | flops 2415919104 | bytes 14155776 | tf_op jit(solution)/shard_map/vrzin,vrnx->vrzix/dot_general | solution.py:202
  125.5 2.5 %convolution_bitcast_fusion.1 = f32[32,64,256]{2,1,0:T(8,128)S(1)} fusion(f32[2,3,32,32,256]{4,3,0,2,1:T(8,128)S(1)} %fusion, f32[2,3,32,64]{3,2,1,0:T(8,128)S(1)} %bitcast.122, f32[2]{0:T(128)S(1)} %pad_maximum_fusion.5), kind=kOutput, calls=%fused_computation.9 | convolution fusion | flops 603992064 | bytes 8437768 | tf_op jit(solution)/shard_map/vrzix,vrim->zmx/dot_general | solution.py:203
  128.1 1.3 collective-permute-start.1
  129.4 3.1 %collective-permute-start = (f32[32,16,256]{2,1,0:T(8,128)S(1)}, f32[32,16,256]{2,1,0:T(8,128)S(1)}, u32[]{:S(2)}, u32[]{:S(2)}) collective-permute-start(f32[32,16,256]{2,1,0:T(8,128)S(1)} %get-tuple-element.18), channel_id=1, source_target_pairs={{0,1},{1,2},{2,3},{3,4},{4,5},{5,6},{6,7},{8,9},{9,10},{10,11},{11... | collective-permute-start | bytes 1572872 | tf_op jit(solution)/shard_map/ppermute | solution.py:210
  132.5 1.5 collective-permute-done
  134.0 1.2 fusion.9
  135.2 37.9 %finish.1 = f32[4,8,32,256]{3,2,1,0:T(8,128)} custom-call(f32[8,4,32,256]{3,2,1,0:T(8,128)} %bitcast.119, f32[4,8,32,256]{3,2,1,0:T(8,128)} %bitcast.115), custom_call_target="tpu_custom_call" | custom-call | tf_op jit(solution)/shard_map/finish/pallas_call | solution.py:132
  173.1 2.3 %copy.68 = f32[4,256,256]{2,1,0:T(8,128)} copy(f32[4,256,256]{2,1,0:T(8,128)} %bitcast.120) | data formatting | bytes 2097152
  (30 shorter events, 0.8 us)
Async XLA Ops:
  9.0 12.0 %all-to-all-start = ((s32[8,4,2]{1,2,0:T(2,128)}), s32[8,4,2]{1,2,0:T(2,128)S(1)}, u32[]{:S(2)}, u32[]{:S(2)}) async-start(s32[8,4,2]{1,2,0:T(2,128)} %copy.14), calls=%async_computation | async-start | bytes 16384 | tf_op jit(solution)/shard_map/all_to_all | solution.py:187
  17.6 6.9 %copy-start = (f32[4,256,256]{2,1,0:T(8,128)S(1)}, f32[4,256,256]{2,1,0:T(8,128)}, u32[]{:S(2)}) copy-start(f32[4,256,256]{2,1,0:T(8,128)} %param.8) | copy-start | bytes 3145732
  20.9 30.1 %all-to-all-start.1 = ((bf16[32,2,32,256]{3,2,1,0:T(8,128)(2,1)}), bf16[32,2,32,256]{3,2,1,0:T(8,128)(2,1)S(1)}, u32[]{:S(2)}, u32[]{:S(2)}) async-start(bf16[32,2,32,256]{3,2,1,0:T(8,128)(2,1)} %copy.18), calls=%async_computation.1 | async-start | bytes 2097152 | tf_op jit(solution)/shard_map/all_to_all | solution.py:186
  51.0 1.0 copy-start.2
  52.0 52.6 %all-to-all-start.2 = ((f32[8,4,64,256]{3,2,1,0:T(8,128)}), f32[8,4,64,256]{3,2,1,0:T(8,128)S(1)}, u32[]{:S(2)}, u32[]{:S(2)}) async-start(f32[8,4,64,256]{3,2,1,0:T(8,128)} %fusion.18), calls=%async_computation.2 | async-start | bytes 4194304 | tf_op jit(solution)/shard_map/all_to_all | solution.py:176
  63.7 40.9 %copy-start.3 = (f32[6,32,64]{2,1,0:T(8,128)S(1)}, f32[6,32,64]{2,1,0:T(8,128)}, u32[]{:S(2)}) copy-start(f32[6,32,64]{2,1,0:T(8,128)} %get-tuple-element.8) | copy-start | bytes 147460
  104.5 2.7 %copy-start.1 = (f32[6,256,256]{2,1,0:T(8,128)S(1)}, f32[6,256,256]{2,1,0:T(8,128)}, u32[]{:S(2)}) copy-start(f32[6,256,256]{2,1,0:T(8,128)} %get-tuple-element.10) | copy-start | bytes 4718596
  107.2 6.4 %copy-start.4 = (f32[6,32,32]{2,1,0:T(8,128)S(1)}, f32[6,32,32]{2,1,0:T(8,128)}, u32[]{:S(2)}) copy-start(f32[6,32,32]{2,1,0:T(8,128)} %get-tuple-element.9) | copy-start | bytes 73732
  128.1 4.4 %collective-permute-start.1 = (f32[32,16,256]{2,1,0:T(8,128)S(1)}, f32[32,16,256]{2,1,0:T(8,128)S(1)}, u32[]{:S(2)}, u32[]{:S(2)}) collective-permute-start(f32[32,16,256]{2,1,0:T(8,128)S(1)} %get-tuple-element.19), channel_id=1, source_target_pairs={{1,0},{2,1},{3,2},{4,3},{5,4},{6,5},{7,6},{9,8},{10,9},{11,10},{12... | collective-permute-start | bytes 1572872 | tf_op jit(solution)/shard_map/ppermute | solution.py:211
  129.4 4.6 %collective-permute-start = (f32[32,16,256]{2,1,0:T(8,128)S(1)}, f32[32,16,256]{2,1,0:T(8,128)S(1)}, u32[]{:S(2)}, u32[]{:S(2)}) collective-permute-start(f32[32,16,256]{2,1,0:T(8,128)S(1)} %get-tuple-element.18), channel_id=1, source_target_pairs={{0,1},{1,2},{2,3},{3,4},{4,5},{5,6},{6,7},{8,9},{9,10},{10,11},{11... | collective-permute-start | bytes 1572872 | tf_op jit(solution)/shard_map/ppermute | solution.py:210

commit v3 on v2

--- a/solution.py
+++ b/solution.py
@@ -41,6 +41,122 @@
     )(*rows_in)
 
 
+def spread_kernel(blocks, groups, step, padded, planes, pencil, got, sa, ra, sb, rb, sp, rp):
+    me = lax.axis_index("blk")
+    grp = lax.axis_index("grp")
+    cz, span = pencil.shape[1], pencil.shape[2]
+    cq = cz // groups
+    mine = pl.ds(grp * cq, cq)
+    barrier = pltpu.get_barrier_semaphore()
+    for k in range(1, groups):
+        pl.semaphore_signal(barrier, inc=1, device_id=(lax.rem(grp + k, groups), me), device_id_type=MESH)
+    for rel in range(1, blocks):
+        pl.semaphore_signal(barrier, inc=1, device_id=(grp, lax.rem(me + rel, blocks)), device_id_type=MESH)
+    pl.semaphore_wait(barrier, groups + blocks - 2)
+
+    first, small, second = {}, {}, {}
+    for rel in range(1, blocks):
+        dest = lax.rem(me + rel, blocks)
+        first[rel] = pltpu.make_async_remote_copy(
+            src_ref=padded.at[mine, pl.ds(dest * step, span)],
+            dst_ref=pencil.at[me, mine],
+            send_sem=sa.at[rel],
+            recv_sem=ra.at[rel],
+            device_id=(grp, dest),
+            device_id_type=MESH,
+        )
+        first[rel].start()
+    for rel in range(1, blocks):
+        dest = lax.rem(me + rel, blocks)
+        small[rel] = pltpu.make_async_remote_copy(
+            src_ref=planes.at[dest],
+            dst_ref=got.at[me],
+            send_sem=sp.at[rel],
+            recv_sem=rp.at[rel],
+            device_id=(grp, dest),
+            device_id_type=MESH,
+        )
+        small[rel].start()
+    pencil[me] = padded[:, pl.ds(me * step, span)]
+    got[me] = planes[me]
+    for rel in range(1, blocks):
+        src = lax.rem(me + blocks - rel, blocks)
+        landed = pencil.at[src, mine]
+        pltpu.make_async_remote_copy(
+            src_ref=landed,
+            dst_ref=landed,
+            send_sem=sa.at[rel],
+            recv_sem=ra.at[rel],
+            device_id=(grp, src),
+            device_id_type=MESH,
+        ).wait_recv()
+        for k in range(1, groups):
+            second[rel, k] = pltpu.make_async_remote_copy(
+                src_ref=landed,
+                dst_ref=landed,
+                send_sem=sb.at[rel, k - 1],
+                recv_sem=rb.at[rel, k - 1],
+                device_id=(lax.rem(grp + k, groups), me),
+                device_id_type=MESH,
+            )
+            second[rel, k].start()
+    for rel in range(1, blocks):
+        src = lax.rem(me + blocks - rel, blocks)
+        for k in range(1, groups):
+            peer = lax.rem(grp + groups - k, groups)
+            theirs = pencil.at[src, pl.ds(peer * cq, cq)]
+            pltpu.make_async_remote_copy(
+                src_ref=theirs,
+                dst_ref=theirs,
+                send_sem=sb.at[rel, k - 1],
+                recv_sem=rb.at[rel, k - 1],
+                device_id=(peer, me),
+                device_id_type=MESH,
+            ).wait_recv()
+        pltpu.make_async_remote_copy(
+            src_ref=planes.at[src],
+            dst_ref=got.at[src],
+            send_sem=sp.at[rel],
+            recv_sem=rp.at[rel],
+            device_id=(grp, src),
+            device_id_type=MESH,
+        ).wait_recv()
+    for copies in (first, small, second):
+        for copy in copies.values():
+            copy.wait_send()
+
+
+def spread(estimate, planes, lead, blocks, groups):
+    cz, ny, nx = estimate.shape
+    py = ny // blocks
+    chunk = min(py, lead)
+    span = (py + 2 * lead) // chunk
+    padded = jnp.pad(estimate, ((0, 0), (lead, lead), (0, 0))).reshape(cz, -1, chunk, nx)
+    vmem = pl.BlockSpec(memory_space=pltpu.VMEM)
+    dma = pltpu.SemaphoreType.DMA
+    pencil, got = pl.pallas_call(
+        lambda *refs: spread_kernel(blocks, groups, py // chunk, *refs),
+        out_shape=[
+            jax.ShapeDtypeStruct((blocks, cz, span, chunk, nx), jnp.float32),
+            jax.ShapeDtypeStruct(planes.shape, jnp.int32),
+        ],
+        in_specs=[vmem, vmem],
+        out_specs=[vmem, vmem],
+        scratch_shapes=[
+            dma((blocks,)),
+            dma((blocks,)),
+            dma((blocks, groups - 1)),
+            dma((blocks, groups - 1)),
+            dma((blocks,)),
+            dma((blocks,)),
+        ],
+        compiler_params=pltpu.CompilerParams(collective_id=1, has_side_effects=True),
+        cost_estimate=pl.CostEstimate(flops=0, bytes_accessed=1 << 26, transcendentals=0),
+        name="spread",
+    )(padded, planes)
+    return pencil.reshape(cz * blocks, py + 2 * lead, nx), got
+
+
 def finish_kernel(blocks, groups, logs, est, out, got1, send2, got2, s1, r1, s2, r2, s3, r3):
     me = lax.axis_index("blk")
     grp = lax.axis_index("grp")
@@ -171,10 +287,6 @@
     chosen = [jnp.sum(p * ids) for p in picked]
     weights = jnp.stack([jnp.sum(p).astype(jnp.float32) / members for p in picked])
 
-    padded = jnp.pad(estimate, ((0, 0), (lead, lead), (0, 0)))
-    windows = jnp.stack([padded[:, j * py : j * py + ext] for j in range(blocks)])
-    pencil = lax.all_to_all(windows, "blk", 0, 0, tiled=True).reshape(nz, ext, nx)
-
     pick = lambda a: jnp.stack([lax.dynamic_index_in_dim(a, c, 0, keepdims=False) for c in chosen])
     pieces, planes, strips = pick(measured), pick(tile_plane), pick(tile_strip)
     hits = (strips[:, :, None] == jnp.arange(blocks, dtype=jnp.int32)).astype(jnp.int32)
@@ -184,7 +296,11 @@
     send_planes = jnp.sum(jnp.where(order, planes[:, None, :], 0), axis=2)
     send = jnp.einsum("vpi,viyx->pvyx", order.astype(jnp.bfloat16), pieces)
     got = lax.all_to_all(send, "blk", 0, 0, tiled=True)
-    got_planes = lax.all_to_all(send_planes.T, "blk", 0, 0, tiled=True)
+
+    table = send_planes.reshape(VSLOT, blocks, per).transpose(1, 0, 2)
+    table = jnp.pad(table, ((0, 0), (0, 8 - VSLOT), (0, 128 - per)))
+    pencil, table = spread(estimate, table, lead, blocks, groups)
+    got_planes = table[:, :VSLOT, :per].transpose(0, 2, 1).reshape(tiles, VSLOT)
     place = (got_planes[None] == jnp.arange(nz, dtype=jnp.int32)[:, None, None]).astype(jnp.bfloat16)
     observed = jnp.einsum("ptv,tvyx->vpyx", place, got).astype(jnp.float32)
 

time: 176 us -> 157 us (0.89)
  waiting for transfers between devices: 62.6 us -> 1.48 us
  Pallas kernels: 40.2 us -> 91.3 us
  starting transfers between devices: 18.1 us -> 10.7 us
  local copies, waits for them, and re-layouts: 18.4 us -> 13.5 us
  matrix products: 25.8 us -> 29.1 us
    pallas_call x0 -> x1, Pallas kernels: none -> 45.8 us  [spread(): pl.pallas_call(lambda *refs: spread_kernel(blocks, groups, py // chunk, *...]
    all_to_all x2 -> x0, waiting for transfers between devices: 40.5 us -> none  [the longest x1 38.8 us: shards(): lax.all_to_all(windows, 'blk', 0, 0, tiled=True).reshape(nz, ext, nx)]
    all_to_all x1, waiting for transfers between devices: 20.7 us -> 0.01 us  [shards(): got = lax.all_to_all(send, 'blk', 0, 0, tiled=True)]
    all_to_all x2 -> x0, starting transfers between devices: 10.1 us -> none  [the longest x1 6.35 us: shards(): got_planes = lax.all_to_all(send_planes.T, 'blk', 0, 0, tiled=True)]
    unnamed x20 -> x13, local copies, waits for them, and re-layouts: 8.94 us -> 2.9 us
    pallas_call x1, Pallas kernels: 37.9 us -> 43.2 us  [finish(): pl.pallas_call(lambda *refs: finish_kernel(blocks, groups, *refs), out_sh...]
    all_to_all x1, starting transfers between devices: 3.56 us -> 6.35 us  [shards(): got = lax.all_to_all(send, 'blk', 0, 0, tiled=True)]
    dot_general x1, matrix products: 2.65 us -> 4.45 us  [shards(): t = jnp.einsum('zmx,vrim->vrzix', pencil, by, precision=HIGH)]
  transfers between devices with their start and end apart: 5 -> 3, of which waited for: 4 -> 1; matrix products, arithmetic and copies ran while one was open for 9% -> 14% of each run, Pallas kernels for 1% -> 31%
where the time goes in v3:
time: 157 us; the launch traced here: 156 us
  Pallas kernels  91.3 us (58%)
  matrix products  29.1 us (19%)
  local copies, waits for them, and re-layouts  13.5 us (9%)
  starting transfers between devices  10.7 us (7%)
  between operations  6.16 us (4%)
  other arithmetic  4.13 us (3%)
    pallas_call x1, Pallas kernels, spread(): pl.pallas_call(lambda *refs: spread_kernel(blocks, groups, py // chunk, *...  45.8 us
    pallas_call x1, Pallas kernels, finish(): pl.pallas_call(lambda *refs: finish_kernel(blocks, groups, *refs), out_sh...  43.2 us
    dot_general x1, matrix products, shards(): a = jnp.einsum('vrzin,vrnx->vrzix', a, bx, precision=HIGH)  6.41 us
    dot_general x1, matrix products, shards(): t = jnp.einsum('vrzix,vrnx->vrzin', t, bx, precision=HIGH)  6.4 us
    all_to_all x1, starting transfers between devices, shards(): got = lax.all_to_all(send, 'blk', 0, 0, tiled=True)  6.35 us
    dot_general x1, matrix products, shards(): t = jnp.einsum('zmx,vrim->vrzix', pencil, by, precision=HIGH)  4.45 us
    dynamic_slice x5, local copies, waits for them, and re-layouts, shards(): lax.dynamic_index_in_dim(a, c, 0, keepdims=False)  4.25 us
    dot_general x1, matrix products, shards(): blurred = jnp.einsum('vrzin,vrpz->vpin', t, bz, precision=HIGH)  4.16 us
  transfers between devices with their start and end apart: 3, of which 1 were waited for; matrix products, arithmetic and copies ran while one was open for 14% of the time, Pallas kernels for 31%

profile of v3, /device:TPU:0, one launch (start us, length us, event | category | flops | bytes accessed | tf_op | source)
XLA Modules:
  0.0 156.4 jit_solution(15234159694856521063)
XLA Ops:
  0.0 0.7 fusion.28
  0.7 0.2 reduce-window.9
  0.8 1.4 fusion.25
  6.3 0.8 constant_dynamic-slice_fusion.5
  7.1 0.8 constant_dynamic-slice_fusion.3
  7.8 0.1 fusion.18
  7.9 0.1 reduce_window_sum.18
  8.0 0.2 select_reduce_fusion.1
  8.2 1.3 constant_dynamic-slice_fusion.1
  9.5 0.3 copy.51
  9.8 0.3 copy.50
  10.1 0.4 convolution_bitcast_fusion.2
  10.5 1.6 copy.22
  12.1 6.4 %all-to-all-start = ((bf16[32,2,32,256]{3,2,1,0:T(8,128)(2,1)}), bf16[32,2,32,256]{3,2,1,0:T(8,128)(2,1)}, u32[]{:S(2)}, u32[]{:S(2)}) async-start(bf16[32,2,32,256]{3,2,1,0:T(8,128)(2,1)} %copy.22), calls=%async_computation | async-start | bytes 2097152 | tf_op jit(solution)/shard_map/all_to_all | solution.py:298
  18.4 0.7 constant_dynamic-slice_fusion.11
  19.1 0.1 pad_slice_fusion
  19.2 0.7 constant_dynamic-slice_fusion.7
  20.0 0.1 pad_slice_fusion.1
  20.1 0.1 select_reduce_fusion
  20.2 0.1 pad_maximum_fusion
  20.3 0.1 pad_maximum_fusion.4
  20.3 0.6 broadcast_in_dim.28.refs_0_
  20.9 0.1 concatenate.17
  21.0 0.6 broadcast_in_dim.29.refs_1_
  21.6 0.6 broadcast_in_dim.30.refs_2_
  22.2 1.1 pad.31
  23.3 0.1 reshape.92
  23.4 0.6 pad.32.refs_1_
  24.0 45.8 %spread.1 = (f32[8,4,4,16,256]{4,3,2,1,0:T(8,128)}, s32[8,8,128]{2,1,0:T(8,128)}) custom-call(f32[4,18,16,256]{3,2,1,0:T(8,128)} %bitcast.100, s32[8,8,128]{2,1,0:T(8,128)} %pad.32.refs_1_), custom_call_target="tpu_custom_call" | custom-call | bytes 67108864 | tf_op jit(solution)/shard_map/spread/pallas_call | solution.py:137
  69.8 0.8 slice_bitcast_fusion
  70.6 0.1 eq.63
  72.6 2.3 %shard_map.82 = (f32[6,256,256]{2,1,0:T(8,128)}, f32[6,32,64]{2,1,0:T(8,128)}, f32[6,32,32]{2,1,0:T(8,128)}) custom-call(f32[6,1,384]{2,1,0:T(1,128)} %broadcast_in_dim.28.refs_0_, f32[6,1,128]{2,1,0:T(1,128)} %broadcast_in_dim.29.refs_1_, f32[6,1,128]{2,1,0:T(1,128)} %broadcast_in_dim.30.refs_2_), custom_call_target="tpu_custom_call" | custom-call | tf_op jit(solution)/shard_map/pallas_call | solution.py:36
  74.9 0.1 pad_maximum_fusion.5
  75.0 4.4 %convolution_bitcast_fusion = f32[2,3,32,32,256]{4,3,2,1,0:T(8,128)S(1)} fusion(f32[2,3,32,64,1]{3,2,4,1,0:T(8,128)} %bitcast.105, f32[32,64,256,1,1]{2,1,0,4,3:T(8,128)} %bitcast.104), kind=kOutput, calls=%fused_computation.4 | convolution fusion | flops 603979776 | bytes 8437760 | tf_op jit(solution)/shard_map/zmx,vrim->vrzix/dot_general | solution.py:313
  79.5 6.4 %fusion.2 = f32[2,3,32,32,256]{4,2,1,3,0:T(8,128)S(1)} fusion(f32[2,3,256,256,1]{3,2,1,4,0:T(8,128)S(1)} %bitcast.98, f32[2,3,32,32,256]{4,3,2,1,0:T(8,128)S(1)} %convolution_bitcast_fusion), kind=kOutput, calls=%fused_computation.2 | convolution fusion | flops 2415919104 | bytes 14155776 | tf_op jit(solution)/shard_map/vrzix,vrnx->vrzin/dot_general | solution.py:314
  85.9 4.2 %fusion.29 = f32[2,32,32,256,1]{3,1,4,2,0:T(8,128)} fusion(f32[2,3,32,32,1]{3,2,1,4,0:T(8,128)S(1)} %bitcast.107, f32[2,3,32,32,256]{4,2,1,3,0:T(8,128)S(1)} %fusion.2), kind=kOutput, calls=%fused_computation.70 | convolution fusion | flops 301989888 | bytes 8413184 | tf_op jit(solution)/shard_map/vrzin,vrpz->vpin/dot_general | solution.py:315
  90.0 2.1 %fusion.13 = bf16[2,32,32,256]{3,1,2,0:T(8,128)(2,1)S(1)} fusion(bf16[32,2,32,256]{3,2,1,0:T(8,128)(2,1)} %all-to-all-done, s32[32,2]{0,1:T(2,128)S(1)} %eq.63), kind=kOutput, calls=%fused_computation.18 | convolution fusion | flops 33556480 | bytes 2097408 | tf_op jit(solution)/shard_map/ptv,tvyx->vpyx/dot_general | solution.py:305
  92.1 0.0 copy-done.1
  92.1 2.7 %fusion.4 = f32[2,3,32,32,256]{4,2,3,1,0:T(8,128)S(1)} fusion(f32[2,3,32,32,1]{3,2,4,1,0:T(8,128)S(1)} %bitcast.108, f32[2,32,32,256,1]{3,1,4,2,0:T(8,128)S(1)} %copy-done.1, bf16[2,32,32,256]{3,1,2,0:T(8,128)(2,1)S(1)} %fusion.13), kind=kOutput, calls=%fused_computation.5 | convolution fusion | flops 303038464 | bytes 9461760 | tf_op jit(solution)/shard_map/vpin,vrpz->vrzin/dot_general | solution.py:317
  94.8 6.4 %fusion = f32[2,3,32,32,256]{4,3,0,2,1:T(8,128)S(1)} fusion(f32[2,3,32,32,256]{4,2,3,1,0:T(8,128)S(1)} %fusion.4, f32[2,3,256,256,1]{3,2,1,0,4:T(8,128)S(1)} %bitcast.99), kind=kOutput, calls=%fused_computation | convolution fusion | flops 2415919104 | bytes 14155776 | tf_op jit(solution)/shard_map/vrzin,vrnx->vrzix/dot_general | solution.py:318
  101.3 2.5 %convolution_bitcast_fusion.1 = f32[32,64,256]{2,1,0:T(8,128)S(1)} fusion(f32[2,3,32,32,256]{4,3,0,2,1:T(8,128)S(1)} %fusion, f32[2,3,32,64]{3,2,1,0:T(8,128)S(1)} %bitcast.106, f32[2]{0:T(128)S(1)} %pad_maximum_fusion.5), kind=kOutput, calls=%fused_computation.9 | convolution fusion | flops 603992064 | bytes 8437768 | tf_op jit(solution)/shard_map/vrzix,vrim->zmx/dot_general | solution.py:319
  103.8 0.1 fusion.27
  103.9 1.3 collective-permute-start.1
  105.2 3.1 %collective-permute-start = (f32[32,16,256]{2,1,0:T(8,128)S(1)}, f32[32,16,256]{2,1,0:T(8,128)S(1)}, u32[]{:S(2)}, u32[]{:S(2)}) collective-permute-start(f32[32,16,256]{2,1,0:T(8,128)S(1)} %get-tuple-element.22), channel_id=1, source_target_pairs={{0,1},{1,2},{2,3},{3,4},{4,5},{5,6},{6,7},{8,9},{9,10},{10,11},{11... | collective-permute-start | bytes 1572872 | tf_op jit(solution)/shard_map/ppermute | solution.py:326
  108.3 1.5 collective-permute-done
  109.7 1.2 fusion.9
  110.9 43.2 %finish.1 = f32[4,8,32,256]{3,2,1,0:T(8,128)} custom-call(f32[8,4,32,256]{3,2,1,0:T(8,128)} %bitcast.101, f32[4,8,32,256]{3,2,1,0:T(8,128)} %bitcast.102), custom_call_target="tpu_custom_call" | custom-call | tf_op jit(solution)/shard_map/finish/pallas_call | solution.py:248
  154.1 2.3 %copy.67 = f32[4,256,256]{2,1,0:T(8,128)} copy(f32[4,256,256]{2,1,0:T(8,128)} %bitcast.103) | data formatting | bytes 2097152
  (22 shorter events, 0.1 us)
Async XLA Ops:
  10.1 12.1 %copy-start.2 = (f32[4,256,256]{2,1,0:T(8,128)S(1)}, f32[4,256,256]{2,1,0:T(8,128)}, u32[]{:S(2)}) copy-start(f32[4,256,256]{2,1,0:T(8,128)} %param.8) | copy-start | bytes 3145732
  12.1 78.0 %all-to-all-start = ((bf16[32,2,32,256]{3,2,1,0:T(8,128)(2,1)}), bf16[32,2,32,256]{3,2,1,0:T(8,128)(2,1)}, u32[]{:S(2)}, u32[]{:S(2)}) async-start(bf16[32,2,32,256]{3,2,1,0:T(8,128)(2,1)} %copy.22), calls=%async_computation | async-start | bytes 2097152 | tf_op jit(solution)/shard_map/all_to_all | solution.py:298
  75.0 4.5 %copy-start = (f32[6,256,256]{2,1,0:T(8,128)S(1)}, f32[6,256,256]{2,1,0:T(8,128)}, u32[]{:S(2)}) copy-start(f32[6,256,256]{2,1,0:T(8,128)} %get-tuple-element.14) | copy-start | bytes 4718596
  79.5 6.4 %copy-start.4 = (f32[6,32,32]{2,1,0:T(8,128)S(1)}, f32[6,32,32]{2,1,0:T(8,128)}, u32[]{:S(2)}) copy-start(f32[6,32,32]{2,1,0:T(8,128)} %get-tuple-element.11) | copy-start | bytes 73732
  90.0 2.1 %copy-start.1 = (f32[2,32,32,256,1]{3,1,4,2,0:T(8,128)S(1)}, f32[2,32,32,256,1]{3,1,4,2,0:T(8,128)}, u32[]{:S(2)}) copy-start(f32[2,32,32,256,1]{3,1,4,2,0:T(8,128)} %fusion.29) | copy-start | bytes 6291460
  94.8 6.4 %copy-start.3 = (f32[6,32,64]{2,1,0:T(8,128)S(1)}, f32[6,32,64]{2,1,0:T(8,128)}, u32[]{:S(2)}) copy-start(f32[6,32,64]{2,1,0:T(8,128)} %get-tuple-element.10) | copy-start | bytes 147460
  103.9 4.4 %collective-permute-start.1 = (f32[32,16,256]{2,1,0:T(8,128)S(1)}, f32[32,16,256]{2,1,0:T(8,128)S(1)}, u32[]{:S(2)}, u32[]{:S(2)}) collective-permute-start(f32[32,16,256]{2,1,0:T(8,128)S(1)} %get-tuple-element.23), channel_id=1, source_target_pairs={{1,0},{2,1},{3,2},{4,3},{5,4},{6,5},{7,6},{9,8},{10,9},{11,10},{12... | collective-permute-start | bytes 1572872 | tf_op jit(solution)/shard_map/ppermute | solution.py:327
  105.2 4.6 %collective-permute-start = (f32[32,16,256]{2,1,0:T(8,128)S(1)}, f32[32,16,256]{2,1,0:T(8,128)S(1)}, u32[]{:S(2)}, u32[]{:S(2)}) collective-permute-start(f32[32,16,256]{2,1,0:T(8,128)S(1)} %get-tuple-element.22), channel_id=1, source_target_pairs={{0,1},{1,2},{2,3},{3,4},{4,5},{5,6},{6,7},{8,9},{9,10},{10,11},{11... | collective-permute-start | bytes 1572872 | tf_op jit(solution)/shard_map/ppermute | solution.py:326

commit v4 on v3

--- a/solution.py
+++ b/solution.py
@@ -41,7 +41,7 @@
     )(*rows_in)
 
 
-def spread_kernel(blocks, groups, step, padded, planes, pencil, got, sa, ra, sb, rb, sp, rp):
+def spread_kernel(blocks, groups, step, padded, planes, tiles, pencil, got, arrived, sa, ra, sb, rb, sp, rp, st, rt):
     me = lax.axis_index("blk")
     grp = lax.axis_index("grp")
     cz, span = pencil.shape[1], pencil.shape[2]
@@ -54,7 +54,7 @@
         pl.semaphore_signal(barrier, inc=1, device_id=(grp, lax.rem(me + rel, blocks)), device_id_type=MESH)
     pl.semaphore_wait(barrier, groups + blocks - 2)
 
-    first, small, second = {}, {}, {}
+    first, small, second, large = {}, {}, {}, {}
     for rel in range(1, blocks):
         dest = lax.rem(me + rel, blocks)
         first[rel] = pltpu.make_async_remote_copy(
@@ -77,6 +77,18 @@
             device_id_type=MESH,
         )
         small[rel].start()
+    for rel in range(1, blocks):
+        dest = lax.rem(me + rel, blocks)
+        large[rel] = pltpu.make_async_remote_copy(
+            src_ref=tiles.at[dest],
+            dst_ref=arrived.at[me],
+            send_sem=st.at[rel],
+            recv_sem=rt.at[rel],
+            device_id=(grp, dest),
+            device_id_type=MESH,
+        )
+        large[rel].start()
+    arrived[me] = tiles[me]
     pencil[me] = padded[:, pl.ds(me * step, span)]
     got[me] = planes[me]
     for rel in range(1, blocks):
@@ -121,12 +133,20 @@
             device_id=(grp, src),
             device_id_type=MESH,
         ).wait_recv()
-    for copies in (first, small, second):
+        pltpu.make_async_remote_copy(
+            src_ref=tiles.at[src],
+            dst_ref=arrived.at[src],
+            send_sem=st.at[rel],
+            recv_sem=rt.at[rel],
+            device_id=(grp, src),
+            device_id_type=MESH,
+        ).wait_recv()
+    for copies in (first, small, second, large):
         for copy in copies.values():
             copy.wait_send()
 
 
-def spread(estimate, planes, lead, blocks, groups):
+def spread(estimate, planes, tiles, lead, blocks, groups):
     cz, ny, nx = estimate.shape
     py = ny // blocks
     chunk = min(py, lead)
@@ -134,27 +154,30 @@
     padded = jnp.pad(estimate, ((0, 0), (lead, lead), (0, 0))).reshape(cz, -1, chunk, nx)
     vmem = pl.BlockSpec(memory_space=pltpu.VMEM)
     dma = pltpu.SemaphoreType.DMA
-    pencil, got = pl.pallas_call(
+    pencil, got, arrived = pl.pallas_call(
         lambda *refs: spread_kernel(blocks, groups, py // chunk, *refs),
         out_shape=[
             jax.ShapeDtypeStruct((blocks, cz, span, chunk, nx), jnp.float32),
             jax.ShapeDtypeStruct(planes.shape, jnp.int32),
+            jax.ShapeDtypeStruct(tiles.shape, tiles.dtype),
         ],
-        in_specs=[vmem, vmem],
-        out_specs=[vmem, vmem],
+        in_specs=[vmem] * 3,
+        out_specs=[vmem] * 3,
         scratch_shapes=[
             dma((blocks,)),
             dma((blocks,)),
             dma((blocks, groups - 1)),
             dma((blocks, groups - 1)),
+            dma((blocks,)),
+            dma((blocks,)),
             dma((blocks,)),
             dma((blocks,)),
         ],
         compiler_params=pltpu.CompilerParams(collective_id=1, has_side_effects=True),
         cost_estimate=pl.CostEstimate(flops=0, bytes_accessed=1 << 26, transcendentals=0),
         name="spread",
-    )(padded, planes)
-    return pencil.reshape(cz * blocks, py + 2 * lead, nx), got
+    )(padded, planes, tiles)
+    return pencil.reshape(cz * blocks, py + 2 * lead, nx), got, arrived
 
 
 def finish_kernel(blocks, groups, logs, est, out, got1, send2, got2, s1, r1, s2, r2, s3, r3):
@@ -280,26 +303,27 @@
     per = tiles // blocks
 
     matches = (view_group == lax.axis_index("grp")).astype(jnp.int32)
-    ranking = jnp.cumsum(matches) - matches
     members = jnp.sum(matches).astype(jnp.float32)
     ids = jnp.arange(view_group.shape[0], dtype=jnp.int32)
+    ranking = jnp.sum(jnp.where(ids[None, :] < ids[:, None], matches[None, :], 0), axis=1)
     picked = [matches * (ranking == s).astype(jnp.int32) for s in range(VSLOT)]
     chosen = [jnp.sum(p * ids) for p in picked]
     weights = jnp.stack([jnp.sum(p).astype(jnp.float32) / members for p in picked])
 
     pick = lambda a: jnp.stack([lax.dynamic_index_in_dim(a, c, 0, keepdims=False) for c in chosen])
     pieces, planes, strips = pick(measured), pick(tile_plane), pick(tile_strip)
-    hits = (strips[:, :, None] == jnp.arange(blocks, dtype=jnp.int32)).astype(jnp.int32)
-    before = jnp.cumsum(hits, axis=1) - hits
-    positions = strips * per + jnp.sum(before * hits, axis=2)
+    number = jnp.arange(tiles, dtype=jnp.int32)
+    earlier = (strips[:, :, None] == strips[:, None, :]) & (number[None, :] < number[:, None])
+    positions = strips * per + jnp.sum(earlier.astype(jnp.int32), axis=2)
     order = positions[:, None, :] == jnp.arange(tiles, dtype=jnp.int32)[None, :, None]
     send_planes = jnp.sum(jnp.where(order, planes[:, None, :], 0), axis=2)
     send = jnp.einsum("vpi,viyx->pvyx", order.astype(jnp.bfloat16), pieces)
-    got = lax.all_to_all(send, "blk", 0, 0, tiled=True)
+    send = send.reshape(blocks, per, VSLOT, py, nx)
 
     table = send_planes.reshape(VSLOT, blocks, per).transpose(1, 0, 2)
     table = jnp.pad(table, ((0, 0), (0, 8 - VSLOT), (0, 128 - per)))
-    pencil, table = spread(estimate, table, lead, blocks, groups)
+    pencil, table, got = spread(estimate, table, send, lead, blocks, groups)
+    got = got.reshape(tiles, VSLOT, py, nx)
     got_planes = table[:, :VSLOT, :per].transpose(0, 2, 1).reshape(tiles, VSLOT)
     place = (got_planes[None] == jnp.arange(nz, dtype=jnp.int32)[:, None, None]).astype(jnp.bfloat16)
     observed = jnp.einsum("ptv,tvyx->vpyx", place, got).astype(jnp.float32)

time: 157 us -> 143 us (0.911)
  Pallas kernels: 91.3 us -> 79.6 us
  starting transfers between devices: 10.7 us -> 5.84 us
  waiting for transfers between devices: 1.48 us -> 6.1 us
  matrix products: 29.1 us -> 27 us
    pallas_call x1, Pallas kernels: 45.8 us -> 38.1 us  [spread(): pl.pallas_call(lambda *refs: spread_kernel(blocks, groups, py // chunk, *...]
    all_to_all x1 -> x0, starting transfers between devices: 6.35 us -> none  [shards(): got = lax.all_to_all(send, 'blk', 0, 0, tiled=True)]
    ppermute x1, waiting for transfers between devices: 0.01 us -> 5.91 us  [shards(): down = lax.ppermute(down, 'blk', [(i, i - d) for i in range(d, blocks)])]
    pallas_call x1, Pallas kernels: 43.2 us -> 39.2 us  [finish(): pl.pallas_call(lambda *refs: finish_kernel(blocks, groups, *refs), out_sh...]
  transfers between devices with their start and end apart: 3 -> 2, of which waited for: 1 -> 2; matrix products, arithmetic and copies ran while one was open for 14% -> 0% of each run, Pallas kernels for 31% -> 0%
where the time goes in v4:
time: 143 us; the launch traced here: 142 us
  Pallas kernels  79.6 us (56%)
  matrix products  27 us (19%)
  local copies, waits for them, and re-layouts  13.8 us (10%)
  waiting for transfers between devices  6.1 us (4%)
  between operations  5.94 us (4%)
  starting transfers between devices  5.84 us (4%)
  other arithmetic  3.95 us (3%)
    pallas_call x1, Pallas kernels, finish(): pl.pallas_call(lambda *refs: finish_kernel(blocks, groups, *refs), out_sh...  39.2 us
    pallas_call x1, Pallas kernels, spread(): pl.pallas_call(lambda *refs: spread_kernel(blocks, groups, py // chunk, *...  38.1 us
    dot_general x1, matrix products, shards(): a = jnp.einsum('vrzin,vrnx->vrzix', a, bx, precision=HIGH)  6.61 us
    dot_general x1, matrix products, shards(): t = jnp.einsum('vrzix,vrnx->vrzin', t, bx, precision=HIGH)  6.56 us
    ppermute x1, waiting for transfers between devices, shards(): down = lax.ppermute(down, 'blk', [(i, i - d) for i in range(d, blocks)])  5.91 us
    ppermute x1, starting transfers between devices, shards(): up = lax.ppermute(up, 'blk', [(i, i + d) for i in range(blocks - d)])  4.55 us
    dynamic_slice x5, local copies, waits for them, and re-layouts, shards(): lax.dynamic_index_in_dim(a, c, 0, keepdims=False)  4.37 us
    dot_general x1, matrix products, shards(): t = jnp.einsum('zmx,vrim->vrzix', pencil, by, precision=HIGH)  3.68 us
  transfers between devices with their start and end apart: 2, of which 2 were waited for; matrix products, arithmetic and copies ran while one was open for 0% of the time, Pallas kernels for 0%

profile of v4, /device:TPU:0, one launch (start us, length us, event | category | flops | bytes accessed | tf_op | source)
XLA Modules:
  0.0 142.2 jit_solution(5256823840954233225)
XLA Ops:
  0.0 0.7 compare_convert_fusion
  0.7 0.1 select_reduce_fusion.1
  0.8 1.4 %fusion.24 = (s32[]{:T(128)}, s32[]{:T(128)}, s32[]{:T(128)}, s32[]{:T(128)}, s32[]{:T(128)}) fusion(s32[6]{0:T(128)S(1)} %select_reduce_fusion.1, s32[6]{0:T(128)} %param.12, s32[]{:T(128)S(6)} %axis_index.15), kind=kLoop, calls=%fused_computation.66 | loop fusion | flops 73 | bytes 72 | tf_op jit(solution)/shard_map/reduce_sum | solution.py:311
  8.0 0.8 constant_dynamic-slice_fusion.3
  8.7 0.8 constant_dynamic-slice_fusion.5
  9.5 0.2 convert_reduce_fusion
  9.7 0.8 constant_dynamic-slice_fusion.11
  10.5 0.1 select_reduce_fusion
  10.6 0.1 reshape.84
  10.7 0.8 constant_dynamic-slice_fusion.7
  11.5 0.1 pad_slice_fusion.1
  11.6 0.1 pad_maximum_fusion.4
  11.7 0.6 broadcast_in_dim.50.refs_2_
  12.3 0.1 concatenate.17
  12.4 0.6 broadcast_in_dim.49.refs_1_
  13.0 0.1 pad_slice_fusion
  13.0 0.1 pad_maximum_fusion
  13.1 0.6 broadcast_in_dim.48.refs_0_
  13.7 0.6 pad.32.refs_1_
  14.3 1.3 constant_dynamic-slice_fusion.1
  15.6 0.0 copy-start.1
  15.6 0.3 copy.56
  15.9 0.3 copy.57
  16.2 0.4 convolution_bitcast_fusion.2
  16.7 1.6 %copy.27 = bf16[32,2,32,256]{3,2,1,0:T(8,128)(2,1)} copy(bf16[32,2,32,256]{3,0,2,1:T(8,128)(2,1)S(1)} %convolution_bitcast_fusion.2) | data formatting | bytes 2097152 | tf_op jit(solution)/shard_map/vpi,viyx->pvyx/transpose | solution.py:320
  18.2 0.0 copy-done.1
  18.2 1.1 pad.31
  19.4 38.1 %spread.1 = (f32[8,4,4,16,256]{4,3,2,1,0:T(8,128)}, s32[8,8,128]{2,1,0:T(8,128)}, bf16[8,4,2,32,256]{4,3,2,1,0:T(8,128)(2,1)}) custom-call(f32[4,18,16,256]{3,2,1,0:T(8,128)} %bitcast.86, s32[8,8,128]{2,1,0:T(8,128)} %pad.32.refs_1_, bf16[8,4,2,32,256]{4,3,2,1,0:T(8,128)(2,1)} %bitcast.90), custom_call_target="tpu_custom_call" | custom-call | bytes 67108864 | tf_op jit(solution)/shard_map/spread/pallas_call | solution.py:157
  57.5 0.9 slice_bitcast_fusion
  58.4 0.1 eq.63
  58.4 0.1 pad_maximum_fusion.5
  58.5 1.9 %fusion.13 = bf16[2,32,32,256]{3,1,2,0:T(8,128)(2,1)S(1)} fusion(bf16[32,2,32,256]{3,2,1,0:T(8,128)(2,1)} %bitcast.92, s32[32,2]{0,1:T(2,128)S(1)} %eq.63), kind=kOutput, calls=%fused_computation.18 | convolution fusion | flops 33556480 | bytes 2097408 | tf_op jit(solution)/shard_map/ptv,tvyx->vpyx/dot_general | solution.py:329
  60.5 2.3 %shard_map.82 = (f32[6,256,256]{2,1,0:T(8,128)}, f32[6,32,64]{2,1,0:T(8,128)}, f32[6,32,32]{2,1,0:T(8,128)}) custom-call(f32[6,1,384]{2,1,0:T(1,128)} %broadcast_in_dim.48.refs_0_, f32[6,1,128]{2,1,0:T(1,128)} %broadcast_in_dim.49.refs_1_, f32[6,1,128]{2,1,0:T(1,128)} %broadcast_in_dim.50.refs_2_), custom_call_target="tpu_custom_call" | custom-call | tf_op jit(solution)/shard_map/pallas_call | solution.py:36
  62.7 3.7 %convolution_bitcast_fusion = f32[2,3,32,32,256]{4,3,2,1,0:T(8,128)S(1)} fusion(f32[2,3,32,64,1]{3,2,4,1,0:T(8,128)} %bitcast.93, f32[32,64,256,1,1]{2,1,0,4,3:T(8,128)S(1)} %bitcast.91), kind=kOutput, calls=%fused_computation.4 | convolution fusion | flops 603979776 | bytes 8437760 | tf_op jit(solution)/shard_map/zmx,vrim->vrzix/dot_general | solution.py:337
  66.4 6.6 %fusion.2 = f32[2,3,32,32,256]{4,2,1,3,0:T(8,128)S(1)} fusion(f32[2,3,256,256,1]{3,2,1,4,0:T(8,128)S(1)} %bitcast.84, f32[2,3,32,32,256]{4,3,2,1,0:T(8,128)S(1)} %convolution_bitcast_fusion), kind=kOutput, calls=%fused_computation.2 | convolution fusion | flops 2415919104 | bytes 14155776 | tf_op jit(solution)/shard_map/vrzix,vrnx->vrzin/dot_general | solution.py:338
  73.0 2.6 %fusion.27 = f32[2,32,32,256,1]{3,1,4,2,0:T(8,128)S(1)} fusion(f32[2,3,32,32,1]{3,2,1,4,0:T(8,128)S(1)} %bitcast.95, f32[2,3,32,32,256]{4,2,1,3,0:T(8,128)S(1)} %fusion.2), kind=kOutput, calls=%fused_computation.69 | convolution fusion | flops 301989888 | bytes 8413184 | tf_op jit(solution)/shard_map/vrzin,vrpz->vpin/dot_general | solution.py:339
  75.6 2.7 %fusion.4 = f32[2,3,32,32,256]{4,2,3,1,0:T(8,128)S(1)} fusion(f32[2,3,32,32,1]{3,2,4,1,0:T(8,128)S(1)} %bitcast.96, f32[2,32,32,256,1]{3,1,4,2,0:T(8,128)S(1)} %fusion.27, bf16[2,32,32,256]{3,1,2,0:T(8,128)(2,1)S(1)} %fusion.13), kind=kOutput, calls=%fused_computation.5 | convolution fusion | flops 303038464 | bytes 9461760 | tf_op jit(solution)/shard_map/vpin,vrpz->vrzin/dot_general | solution.py:341
  78.3 0.0 copy-start.3
  78.3 6.6 %fusion = f32[2,3,32,32,256]{4,3,0,2,1:T(8,128)S(1)} fusion(f32[2,3,32,32,256]{4,2,3,1,0:T(8,128)S(1)} %fusion.4, f32[2,3,256,256,1]{3,2,1,0,4:T(8,128)S(1)} %bitcast.85), kind=kOutput, calls=%fused_computation | convolution fusion | flops 2415919104 | bytes 14155776 | tf_op jit(solution)/shard_map/vrzin,vrnx->vrzix/dot_general | solution.py:342
  85.0 2.5 %convolution_bitcast_fusion.1 = f32[32,64,256]{2,1,0:T(8,128)S(1)} fusion(f32[2,3,32,32,256]{4,3,0,2,1:T(8,128)S(1)} %fusion, f32[2,3,32,64]{3,2,1,0:T(8,128)S(1)} %bitcast.94, f32[2]{0:T(128)S(1)} %pad_maximum_fusion.5), kind=kOutput, calls=%fused_computation.9 | convolution fusion | flops 603992064 | bytes 8437768 | tf_op jit(solution)/shard_map/vrzix,vrim->zmx/dot_general | solution.py:343
  87.5 0.1 fusion.26
  87.6 4.6 %collective-permute-start = (f32[32,16,256]{2,1,0:T(8,128)S(1)}, f32[32,16,256]{2,1,0:T(8,128)S(1)}, u32[]{:S(2)}, u32[]{:S(2)}) collective-permute-start(f32[32,16,256]{2,1,0:T(8,128)S(1)} %get-tuple-element.24), channel_id=1, source_target_pairs={{0,1},{1,2},{2,3},{3,4},{4,5},{5,6},{6,7},{8,9},{9,10},{10,11},{11... | collective-permute-start | bytes 1572872 | tf_op jit(solution)/shard_map/ppermute | solution.py:350
  92.1 1.3 collective-permute-start.1
  93.4 0.2 collective-permute-done
  93.6 5.9 %collective-permute-done.1 = f32[32,16,256]{2,1,0:T(8,128)S(1)} collective-permute-done((f32[32,16,256]{2,1,0:T(8,128)S(1)}, f32[32,16,256]{2,1,0:T(8,128)S(1)}, u32[]{:S(2)}, u32[]{:S(2)}) %collective-permute-start.1) | collective-permute-done | bytes 524320 | tf_op jit(solution)/shard_map/ppermute | solution.py:351
  99.5 1.2 fusion.9
  100.7 39.2 %finish.1 = f32[4,8,32,256]{3,2,1,0:T(8,128)} custom-call(f32[8,4,32,256]{3,2,1,0:T(8,128)} %bitcast.87, f32[4,8,32,256]{3,2,1,0:T(8,128)} %bitcast.88), custom_call_target="tpu_custom_call" | custom-call | tf_op jit(solution)/shard_map/finish/pallas_call | solution.py:271
  139.9 2.3 %copy.73 = f32[4,256,256]{2,1,0:T(8,128)} copy(f32[4,256,256]{2,1,0:T(8,128)} %bitcast.89) | data formatting | bytes 2097152
  (19 shorter events, 0.1 us)
Async XLA Ops:
  15.6 2.6 %copy-start.1 = (f32[4,256,256]{2,1,0:T(8,128)S(1)}, f32[4,256,256]{2,1,0:T(8,128)}, u32[]{:S(2)}) copy-start(f32[4,256,256]{2,1,0:T(8,128)} %param.8) | copy-start | bytes 3145732
  57.4 5.3 %copy-start.2 = (f32[8,4,4,16,256]{4,3,2,1,0:T(8,128)S(1)}, f32[8,4,4,16,256]{4,3,2,1,0:T(8,128)}, u32[]{:S(2)}) copy-start(f32[8,4,4,16,256]{4,3,2,1,0:T(8,128)} %get-tuple-element.15) | copy-start | bytes 6291460
  62.7 3.7 %copy-start = (f32[6,256,256]{2,1,0:T(8,128)S(1)}, f32[6,256,256]{2,1,0:T(8,128)}, u32[]{:S(2)}) copy-start(f32[6,256,256]{2,1,0:T(8,128)} %get-tuple-element.16) | copy-start | bytes 4718596
  66.4 6.6 %copy-start.4 = (f32[6,32,32]{2,1,0:T(8,128)S(1)}, f32[6,32,32]{2,1,0:T(8,128)}, u32[]{:S(2)}) copy-start(f32[6,32,32]{2,1,0:T(8,128)} %get-tuple-element.12) | copy-start | bytes 73732
  78.3 6.6 %copy-start.3 = (f32[6,32,64]{2,1,0:T(8,128)S(1)}, f32[6,32,64]{2,1,0:T(8,128)}, u32[]{:S(2)}) copy-start(f32[6,32,64]{2,1,0:T(8,128)} %get-tuple-element.11) | copy-start | bytes 147460
  87.6 6.0 %collective-permute-start = (f32[32,16,256]{2,1,0:T(8,128)S(1)}, f32[32,16,256]{2,1,0:T(8,128)S(1)}, u32[]{:S(2)}, u32[]{:S(2)}) collective-permute-start(f32[32,16,256]{2,1,0:T(8,128)S(1)} %get-tuple-element.24), channel_id=1, source_target_pairs={{0,1},{1,2},{2,3},{3,4},{4,5},{5,6},{6,7},{8,9},{9,10},{10,11},{11... | collective-permute-start | bytes 1572872 | tf_op jit(solution)/shard_map/ppermute | solution.py:350
  92.1 7.4 %collective-permute-start.1 = (f32[32,16,256]{2,1,0:T(8,128)S(1)}, f32[32,16,256]{2,1,0:T(8,128)S(1)}, u32[]{:S(2)}, u32[]{:S(2)}) collective-permute-start(f32[32,16,256]{2,1,0:T(8,128)S(1)} %get-tuple-element.25), channel_id=1, source_target_pairs={{1,0},{2,1},{3,2},{4,3},{5,4},{6,5},{7,6},{9,8},{10,9},{11,10},{12... | collective-permute-start | bytes 1572872 | tf_op jit(solution)/shard_map/ppermute | solution.py:351
